TPU v7x, 32 devices: a whole 2x2x4 slice. The times are simulated.
32 devices in a mesh: chan: 4 (over z), slab: 2 (over core), batch: 4 (over y, x).
Axes of the slice: x: 2, y: 2, z: 4, core: 2. Of those that a mesh axis runs over, the one named last changes fastest.
Arguments:
- inputs: bfloat16 [2048, 8, 512], P(('batch', 'chan'), 'slab'), parts along dimension 0, may hold values from -6 to 6
- weights: bfloat16 [27, 512, 512], P(None, 'chan'), may hold values from -0.0625 to 0.0625
- out_grad: bfloat16 [2048, 8, 512], P(('batch', 'chan'), 'slab'), parts along dimension 0, may hold values from -6 to 6
Outputs:
- conv_out: bfloat16 [2048, 8, 512], P(('batch', 'chan'), 'slab'), parts along dimension 0
- input_grad: bfloat16 [2048, 8, 512], P(('batch', 'chan'), 'slab'), parts along dimension 0
There are 4 independent parts, one for each index of `batch`. A program takes and returns all parts, laid end to end along the dimension named above; an argument that names none is the same for every part. Nothing has to cross between parts.
All inputs are finite; a program needn't handle non-finite values.
Results may differ from a plain program's by a relative error of at most 0.0013.
Values may be sent and summed in bfloat16 or wider, within the bound.
No kernel may reach another device: no remote copies, remote signals or barrier semaphores. Data moves between devices by JAX's collectives and lax.ppermute only.
A program may use at most 192 MiB of HBM per device.

v0:
```python
import functools

import jax
import jax.numpy as jnp
from jax import lax
from jax.experimental import pallas as pl
from jax.experimental.pallas import tpu as pltpu
from jax.sharding import PartitionSpec as P

NZ = 64
OFFSETS = (-1, 0, 1)
VMEM_LIMIT = 56 * 2**20

def shift_z(block, offset):
    if offset == 0:
        return block
    lanes = block.shape[1]
    z = lax.broadcasted_iota(jnp.int32, block.shape, 1) % NZ
    plain = pltpu.roll(block, offset % lanes, 1)
    wrapped = pltpu.roll(block, (offset - NZ * offset) % lanes, 1)
    edge = z == (0 if offset == 1 else NZ - 1)
    return jnp.where(edge, wrapped, plain)

def shift_y(block, offset):
    if offset == 0:
        return block
    return pltpu.roll(block, (NZ * offset) % block.shape[1], 1)

def forward_kernel(slab, halo_ref, x_ref, w_ref, out_ref, columns, wt):
    plane = pl.program_id(0)
    chans, size = w_ref.shape[1], out_ref.shape[1]

    @pl.when(plane == 0)
    def _():
        for o in range(27):
            wt[:, o * chans:(o + 1) * chans] = w_ref[o].T
        for p in range(slab + 2):
            if p == 0:
                source = halo_ref[:, :size]
            elif p == slab + 1:
                source = halo_ref[:, size:]
            else:
                source = x_ref[:, (p - 1) * size:p * size]
            for iz, offset_z in enumerate(OFFSETS):
                moved = shift_z(source, -offset_z)
                for iy, offset_y in enumerate(OFFSETS):
                    row = (3 * iy + iz) * chans
                    columns[row:row + chans, p * size:(p + 1) * size] = shift_y(moved, -offset_y)

    total = None
    for ix in range(3):
        at = pl.multiple_of((plane + ix) * size, size)
        part = jnp.dot(wt[:, ix * 9 * chans:(ix + 1) * 9 * chans], columns[:, pl.ds(at, size)],
                       preferred_element_type=jnp.float32)
        total = part if total is None else total + part
    out_ref[...] = total

def forward(x, halo, w, slab):
    chans, cells = x.shape
    size = cells // slab
    full = w.shape[2]
    whole = lambda a: pl.BlockSpec(a.shape, lambda n: (0,) * a.ndim, pipeline_mode=pl.Buffered(1))
    return pl.pallas_call(
        functools.partial(forward_kernel, slab),
        grid=(slab,),
        in_specs=[whole(halo), whole(x), whole(w)],
        out_specs=pl.BlockSpec((full, size), lambda n: (0, n)),
        out_shape=jax.ShapeDtypeStruct((full, cells), jnp.float32),
        scratch_shapes=[pltpu.VMEM((9 * chans, (slab + 2) * size), jnp.bfloat16),
                        pltpu.VMEM((full, 27 * chans), jnp.bfloat16)],
        compiler_params=pltpu.CompilerParams(vmem_limit_bytes=VMEM_LIMIT),
        cost_estimate=pl.CostEstimate(flops=2*27*chans*full*cells, bytes_accessed=w.size*2+full*cells*4, transcendentals=0),
        name="forward",
    )(halo, x, w)

def backward_kernel(slab, number, first, where_ref, *refs):
    halos, blocks = refs[:number], refs[number:2 * number]
    w_ref = refs[2 * number]
    before = None if first else refs[2 * number + 1]
    out_ref, lhs, rhs = refs[-3:]
    plane = pl.program_id(0)
    chans_in, size = w_ref.shape[1], out_ref.shape[1]
    chans = blocks[0].shape[0]

    @pl.when(plane == 0)
    def _():
        for k in range(number):
            at = pl.multiple_of(where_ref[k] * chans, chans)
            for ix, offset_x in enumerate(OFFSETS):
                row = (3 * k + ix) * chans
                for o in range(9):
                    lhs[o * chans_in:(o + 1) * chans_in, row:row + chans] = w_ref[9 * ix + o, :, pl.ds(at, chans)]
                if offset_x == 0:
                    rhs[row:row + chans, :] = blocks[k][...]
                elif offset_x == 1:
                    rhs[row:row + chans, :size] = halos[k][:, :size]
                    rhs[row:row + chans, size:] = blocks[k][:, :(slab - 1) * size]
                else:
                    rhs[row:row + chans, :(slab - 1) * size] = blocks[k][:, size:]
                    rhs[row:row + chans, (slab - 1) * size:] = halos[k][:, size:]

    at = pl.multiple_of(plane * size, size)
    total = None if first else before[...]
    for iz, offset_z in enumerate(OFFSETS):
        over_y = None
        for iy, offset_y in enumerate(OFFSETS):
            row = (3 * iy + iz) * chans_in
            part = jnp.dot(lhs[row:row + chans_in, :], rhs[:, pl.ds(at, size)], preferred_element_type=jnp.float32)
            part = shift_y(part, offset_y)
            over_y = part if over_y is None else over_y + part
        over_y = shift_z(over_y, offset_z)
        total = over_y if total is None else total + over_y
    out_ref[...] = total.astype(out_ref.dtype)

def backward(where, blocks, halos, w, before, slab, out_dtype):
    number = len(blocks)
    chans, cells = blocks[0].shape
    chans_in = w.shape[1]
    size = cells // slab
    first = before is None
    whole = lambda a: pl.BlockSpec(a.shape, lambda n, s: (0,) * a.ndim, pipeline_mode=pl.Buffered(1))
    each = pl.BlockSpec((chans_in, size), lambda n, s: (0, n))
    args = (*halos, *blocks, w) + (() if first else (before,))
    return pl.pallas_call(
        functools.partial(backward_kernel, slab, number, first),
        grid_spec=pltpu.PrefetchScalarGridSpec(
            num_scalar_prefetch=1, grid=(slab,),
            in_specs=[whole(a) for a in args[:2 * number + 1]] + ([] if first else [each]),
            out_specs=each,
            scratch_shapes=[pltpu.VMEM((9 * chans_in, 3 * number * chans), jnp.bfloat16),
                            pltpu.VMEM((3 * number * chans, cells), jnp.bfloat16)]),
        out_shape=jax.ShapeDtypeStruct((chans_in, cells), out_dtype),
        compiler_params=pltpu.CompilerParams(vmem_limit_bytes=VMEM_LIMIT),
        cost_estimate=pl.CostEstimate(flops=2*27*chans*chans_in*cells*number, bytes_accessed=w.size*2+chans_in*cells*4, transcendentals=0),
        name="backward",
    )(where, *args)


def padded(block, sides, width):
    for axis, dim in sides:
        count = lax.axis_size(axis)
        forward_ring = [(i, (i + 1) % count) for i in range(count)]
        backward_ring = [(target, source) for source, target in forward_ring]
        low = lax.ppermute(
            lax.slice_in_dim(block, block.shape[dim] - width, None, axis=dim), axis, forward_ring
        )
        high = lax.ppermute(lax.slice_in_dim(block, 0, width, axis=dim), axis, backward_ring)
        block = jnp.concatenate([low, block, high], axis=dim)
    return block


def stack_yz(block, rows_y):
    chans, slab_len, plane_size = block.shape
    shaped = block.reshape(chans, slab_len, rows_y, NZ)
    pieces = []
    for offset_y in OFFSETS:
        for offset_z in OFFSETS:
            pieces.append(jnp.roll(shaped, (-offset_y, -offset_z), axis=(2, 3)))
    return jnp.stack(pieces).reshape(9 * chans, slab_len * plane_size)


def general(inputs, weights, out_grad):
    chans_in, slab_len, plane_size = inputs.shape
    chans_out = out_grad.shape[0]
    full_out = weights.shape[2]
    rows_y = plane_size // NZ
    cell_count = slab_len * plane_size
    halo_in = padded(inputs, (("slab", 1),), 1)
    grad_all = lax.all_gather(out_grad, "chan", axis=0, tiled=True)
    halo_grad = padded(grad_all, (("slab", 1),), 1)
    running = jnp.zeros((full_out, cell_count), jnp.float32)
    for index_x, offset_x in enumerate(OFFSETS):
        columns = stack_yz(halo_in[:, 1 + offset_x : 1 + offset_x + slab_len], rows_y)
        weight_x = weights[9 * index_x : 9 * index_x + 9].reshape(9 * chans_in, full_out)
        running = running + lax.dot_general(
            weight_x, columns, (((0,), (0,)), ((), ())), preferred_element_type=jnp.float32
        )
    own_rows = lax.psum_scatter(running, "chan", scatter_dimension=0, tiled=True)
    conv_out = own_rows.astype(jnp.bfloat16).reshape(chans_out, slab_len, plane_size)
    running_grad = jnp.zeros((chans_in, slab_len, rows_y, NZ), jnp.float32)
    for index_x, offset_x in enumerate(OFFSETS):
        plane_x = halo_grad[:, 1 - offset_x : 1 - offset_x + slab_len].reshape(full_out, cell_count)
        weight_x = weights[9 * index_x : 9 * index_x + 9].reshape(9 * chans_in, full_out)
        product = lax.dot_general(
            weight_x, plane_x, (((1,), (0,)), ((), ())), preferred_element_type=jnp.float32
        )
        product = product.reshape(9, chans_in, slab_len, rows_y, NZ)
        for index_y, offset_y in enumerate(OFFSETS):
            for index_z, offset_z in enumerate(OFFSETS):
                running_grad = running_grad + jnp.roll(
                    product[3 * index_y + index_z], (offset_y, offset_z), axis=(2, 3)
                )
    input_grad = running_grad.reshape(chans_in, slab_len, plane_size).astype(jnp.bfloat16)
    return (conv_out, input_grad)


def edge_planes(block, size):
    count = lax.axis_size("slab")
    first, last = block[:, :size], block[:, block.shape[1] - size :]
    upward = [(i, (i + 1) % count) for i in range(count)]
    if count <= 2:
        return lax.ppermute(jnp.concatenate([last, first], axis=1), "slab", upward)
    downward = [(target, source) for source, target in upward]
    low, high = lax.ppermute(last, "slab", upward), lax.ppermute(first, "slab", downward)
    return jnp.concatenate([low, high], axis=1)


MARK_ROWS = 8


def pack(total):
    top = jnp.max(jnp.abs(total))
    power = jnp.clip(jnp.ceil(jnp.log2(jnp.maximum(top, 1e-36))), -100.0, 100.0)
    scaled = (total * jnp.exp2(15.0 - power)).astype(jnp.float16)
    mark = jnp.full((MARK_ROWS, total.shape[1]), power, jnp.float16)
    return jnp.concatenate([scaled, mark], axis=0)


def unpack(parcel):
    rows = parcel.shape[0] - MARK_ROWS
    power = parcel[rows, 0].astype(jnp.float32)
    return parcel[:rows].astype(jnp.float32) * jnp.exp2(power - 15.0)


def line_of_four(inputs, weights, out_grad):
    chans, slab_len, size = inputs.shape
    cells = slab_len * size
    place = lax.axis_index("chan")
    move = lambda a, pairs: lax.ppermute(a, "chan", pairs)
    pick = lambda *options: jnp.asarray(options, jnp.int32)[place]
    middle = (place == 1) | (place == 2)

    grad = out_grad.reshape(chans, cells)
    field = inputs.reshape(chans, cells)
    from_below = move(grad, [(0, 1), (1, 2), (2, 3)])
    from_above = move(grad, [(1, 0), (2, 1), (3, 2)])
    field_edges = edge_planes(field, size)
    grad_edges = edge_planes(grad, size)

    partial = forward(field, field_edges, weights, slab_len)
    block = lambda index: lax.dynamic_slice_in_dim(partial, index * chans, chans, axis=0)

    sum_1 = move(pack(block(pick(3, 3, 0, 0))), [(0, 1), (3, 2)])
    below_2 = move(from_below, [(1, 2), (2, 3)])
    above_2 = move(from_above, [(2, 1), (1, 0)])
    second = jnp.where(place == 0, from_above, from_below)
    second_edges = edge_planes(second, size)
    grad_half = backward(
        jnp.stack([place, pick(1, 0, 1, 2)]), (grad, second), (grad_edges, second_edges),
        weights, None, slab_len, jnp.float32,
    )

    parcel = pack(block(pick(2, 3, 0, 1)) + unpack(sum_1))
    sum_below = move(parcel, [(0, 1), (1, 2)])
    sum_above = move(parcel, [(3, 2), (2, 1)])
    relayed = jnp.where(place >= 2, below_2, above_2)
    far = move(relayed, [(2, 3), (1, 0)])
    third = jnp.where(middle, from_above, relayed)
    fourth = jnp.where(middle, relayed, far)
    third_edges = edge_planes(third, size)
    fourth_edges = edge_planes(fourth, size)

    last_below = move(pack(block(pick(1, 2, 3, 3)) + unpack(sum_below)), [(0, 1), (1, 2), (2, 3)])
    last_above = move(pack(block(pick(0, 0, 1, 2)) + unpack(sum_above)), [(3, 2), (2, 1), (1, 0)])
    input_grad = backward(
        jnp.stack([pick(2, 2, 3, 1), pick(3, 3, 0, 0)]), (third, fourth), (third_edges, fourth_edges),
        weights, grad_half, slab_len, jnp.bfloat16,
    )
    conv_out = (block(place) + unpack(last_below) + unpack(last_above)).astype(jnp.bfloat16)
    shape = (chans, slab_len, size)
    return conv_out.reshape(shape), input_grad.reshape(shape)


def per_device(inputs, weights, out_grad):
    chans, size = inputs.shape[0], inputs.shape[2]
    line = lax.axis_size("chan") == 4 and weights.shape[2] == 4 * chans and out_grad.shape[0] == chans
    if line and chans % 128 == 0 and size % 128 == 0:
        return line_of_four(inputs, weights, out_grad)
    return general(inputs, weights, out_grad)


def solution(mesh):
    in_specs = (
        P(("batch", "chan"), "slab", None),
        P(None, "chan", None),
        P(("batch", "chan"), "slab", None),
    )
    out_specs = (P(("batch", "chan"), "slab", None), P(("batch", "chan"), "slab", None))
    return jax.shard_map(
        per_device, mesh=mesh, in_specs=in_specs, out_specs=out_specs, check_vma=False
    )
```

profile of v0, /device:TPU:0, one launch (start us, length us, event | category | flops | bytes accessed | tf_op | source)
XLA Modules:
  0.0 122.6 jit_solution(8557096128532676080)
XLA Ops:
  0.6 1.1 copy.12
  1.8 0.0 copy-start.3
  1.8 0.6 collective-permute-start
  2.4 1.3 %dynamic_slice.41 = s32[1]{0:T(128)} dynamic-slice(s32[4]{0:T(128)} %constant.65.clone, s32[]{:T(128)S(6)} %select_n.49), dynamic_slice_sizes={1} | dynamic-slice | bytes 12 | tf_op jit(solution)/shard_map/dynamic_slice | solution.py:230
  4.3 0.0 copy-start.6
  4.3 0.0 collective-permute-done.halo_ref
  4.3 0.0 copy-start.10
  4.4 0.7 copy-done.10
  5.0 15.3 %forward.1 = f32[512,2048]{1,0:T(8,128)} custom-call(bf16[128,1024]{1,0:T(8,128)(2,1)} %copy-done.10, bf16[128,2048]{1,0:T(8,128)(2,1)} %bitcast.19, bf16[27,128,512]{2,1,0:T(8,128)(2,1)} %refs_4_.3), custom_call_target="tpu_custom_call" | custom-call | flops 7247757312 | bytes 7733248 | tf_op jit(solution)/shard_map/forward/pallas_call | solution.py:63
  20.4 0.0 copy-start.12
  20.4 2.0 %abs_reduce_fusion.3 = f32[]{:T(128)} fusion(f32[512,2048]{1,0:T(8,128)} %forward.1, s32[]{:T(128)S(6)} %select_n.52), kind=kLoop, calls=%fused_computation.11 | loop fusion | flops 524287 | bytes 1048584 | tf_op jit(solution)/shard_map/reduce_max | solution.py:212
  23.1 1.3 %multiply_convert_fusion.3 = f16[128,2048]{1,0:T(8,128)(2,1)S(1)} fusion(f32[512,2048]{1,0:T(8,128)} %forward.1, s32[]{:T(128)S(6)} %select_n.52, f32[]{:T(128)S(6)} %exp2.75), kind=kLoop, calls=%fused_computation.10 | loop fusion | flops 524288 | bytes 1572872 | tf_op jit(solution)/shard_map/convert_element_type | solution.py:214
  24.4 0.1 concatenate.28
  24.5 4.6 %collective-permute-start.1 = (f16[136,2048]{1,0:T(8,128)(2,1)S(1)}, f16[136,2048]{1,0:T(8,128)(2,1)S(1)}, u32[]{:S(2)}, u32[]{:S(2)}) collective-permute-start(f16[136,2048]{1,0:T(8,128)(2,1)S(1)} %concatenate.28), channel_id=1, source_target_pairs={{0,8},{24,16},{1,9},{25,17},{2,10},{26,18},{3,11},{27,19},{4,12},{... | collective-permute-start | bytes 1671176 | tf_op jit(solution)/shard_map/ppermute | solution.py:229
  29.1 0.1 copy.13
  29.2 1.3 %collective-permute-start.7 = (bf16[128,2048]{1,0:T(8,128)(2,1)S(1)}, bf16[128,2048]{1,0:T(8,128)(2,1)S(1)}, u32[]{:S(2)}, u32[]{:S(2)}) collective-permute-start(bf16[128,2048]{1,0:T(8,128)(2,1)S(1)} %bitcast.14), channel_id=1, source_target_pairs={{0,8},{8,16},{16,24},{1,9},{9,17},{17,25},{2,10},{10,18},{18,26},{... | collective-permute-start | bytes 1572872 | tf_op jit(solution)/shard_map/ppermute | solution.py:229
  30.6 1.3 %collective-permute-start.6 = (bf16[128,2048]{1,0:T(8,128)(2,1)S(1)}, bf16[128,2048]{1,0:T(8,128)(2,1)S(1)}, u32[]{:S(2)}, u32[]{:S(2)}) collective-permute-start(bf16[128,2048]{1,0:T(8,128)(2,1)S(1)} %bitcast.15), channel_id=1, source_target_pairs={{8,0},{16,8},{24,16},{9,1},{17,9},{25,17},{10,2},{18,10},{26,18},{... | collective-permute-start | bytes 1572872 | tf_op jit(solution)/shard_map/ppermute | solution.py:229
  31.9 0.2 collective-permute-start.13
  32.1 0.6 dynamic_slice.37
  33.4 0.6 dynamic_slice.39
  34.7 0.6 dynamic_slice.43
  35.9 0.6 dynamic_slice.45
  36.6 0.6 dynamic_slice.47
  37.2 2.4 %pad_add_fusion = (s32[2]{0:T(128)}, s32[2]{0:T(128)}) fusion(s32[1]{0:T(128)} %dynamic_slice.41, s32[1]{0:T(128)} %dynamic_slice.45, s32[1]{0:T(128)} %dynamic_slice.47, s32[1]{0:T(128)} %bitcast.9), kind=kLoop, calls=%fused_computation.21 | loop fusion | flops 4 | bytes 32 | tf_op jit(solution)/shard_map/stack | solution.py:266
  39.6 13.2 %collective-permute-done.7 = bf16[128,2048]{1,0:T(8,128)(2,1)S(1)} collective-permute-done((bf16[128,2048]{1,0:T(8,128)(2,1)S(1)}, bf16[128,2048]{1,0:T(8,128)(2,1)S(1)}, u32[]{:S(2)}, u32[]{:S(2)}) %collective-permute-start.7) | collective-permute-done | bytes 524320 | tf_op jit(solution)/shard_map/ppermute | solution.py:229
  52.8 0.7 collective-permute-start.8
  53.5 0.0 copy-start.8
  53.5 1.3 %collective-permute-start.9 = (bf16[128,2048]{1,0:T(8,128)(2,1)S(1)}, bf16[128,2048]{1,0:T(8,128)(2,1)}, u32[]{:S(2)}, u32[]{:S(2)}) collective-permute-start(bf16[128,2048]{1,0:T(8,128)(2,1)S(1)} %collective-permute-done.6), channel_id=1, source_target_pairs={{16,8},{8,0},{17,9},{9,1},{18,10},{10,2},{19,11},{11,3},{20,12},{1... | collective-permute-start | bytes 1572872 | tf_op jit(solution)/shard_map/ppermute | solution.py:229
  54.8 0.0 collective-permute-done.1
  54.8 0.5 slice.83
  56.0 2.0 %abs_reduce_fusion.2 = f32[]{:T(128)} fusion(f32[512,2048]{1,0:T(8,128)} %forward.1, s32[]{:T(128)S(6)} %select_n.51, f32[]{:T(128)} %bitcast.3, f16[136,2048]{1,0:T(8,128)(2,1)S(1)} %collective-permute-done.1), kind=kLoop, calls=%fused_computation.8 | loop fusion | flops 1310719 | bytes 1572876 | tf_op jit(solution)/shard_map/reduce_max | solution.py:212
  58.8 1.6 %multiply_convert_fusion.2 = f16[128,2048]{1,0:T(8,128)(2,1)S(1)} fusion(f32[512,2048]{1,0:T(8,128)} %forward.1, s32[]{:T(128)S(6)} %select_n.51, f32[]{:T(128)S(6)} %exp2.80, f32[]{:T(128)} %bitcast.3, f16[136,2048]{1,0:T(8,128)(2,1)S(1)} %collective-permute-done.1), kind=kLoop, calls=%fused_computation.7 | loop fusion | flops 1310720 | bytes 2097164 | tf_op jit(solution)/shard_map/convert_element_type | solution.py:214
  60.4 0.1 concatenate.29
  60.5 5.7 %collective-permute-start.2 = (f16[136,2048]{1,0:T(8,128)(2,1)S(1)}, f16[136,2048]{1,0:T(8,128)(2,1)S(1)}, u32[]{:S(2)}, u32[]{:S(2)}) collective-permute-start(f16[136,2048]{1,0:T(8,128)(2,1)S(1)} %concatenate.29), channel_id=1, source_target_pairs={{0,8},{8,16},{1,9},{9,17},{2,10},{10,18},{3,11},{11,19},{4,12},{12... | collective-permute-start | bytes 1671176 | tf_op jit(solution)/shard_map/ppermute | solution.py:229
  66.2 0.7 collective-permute-start.4
  66.9 0.0 copy-start.9
  66.9 0.8 copy-done.9
  67.7 2.6 %collective-permute-done.9 = bf16[128,2048]{1,0:T(8,128)(2,1)} collective-permute-done((bf16[128,2048]{1,0:T(8,128)(2,1)S(1)}, bf16[128,2048]{1,0:T(8,128)(2,1)}, u32[]{:S(2)}, u32[]{:S(2)}) %collective-permute-start.9) | collective-permute-done | bytes 524320 | tf_op jit(solution)/shard_map/ppermute | solution.py:229
  70.3 1.3 %broadcast_select_fusion.3 = (bf16[128,2048]{1,0:T(8,128)(2,1)S(1)}, bf16[128,2048]{1,0:T(8,128)(2,1)S(1)}, bf16[128,2048]{1,0:T(8,128)(2,1)S(1)}) fusion(bf16[128,2048]{1,0:T(8,128)(2,1)} %copy-done.8, pred[]{:T(512)S(6)} %or.3, bf16[128,2048]{1,0:T(8,128)(2,1)} %copy-done.9, bf16[128,2048]{1,0:T(8,128)(2,1)} %collective-permute-done.9, pred[]{:T(512)S(6)} %ge.3, ...), kind=kLoop, calls=%fused_computation.15 | loop fusion | flops 786432 | bytes 3670019 | tf_op jit(solution)/shard_map/jit(_where)/select_n | solution.py:258
  71.6 0.0 copy-start.4
  71.7 0.8 pad_maximum_fusion.1
  72.5 1.3 %collective-permute-start.11 = (bf16[128,2048]{1,0:T(8,128)(2,1)S(1)}, bf16[128,2048]{1,0:T(8,128)(2,1)S(1)}, u32[]{:S(2)}, u32[]{:S(2)}) collective-permute-start(bf16[128,2048]{1,0:T(8,128)(2,1)S(1)} %get-tuple-element.5), channel_id=1, source_target_pairs={{16,24},{8,0},{17,25},{9,1},{18,26},{10,2},{19,27},{11,3},{20,28},... | collective-permute-start | bytes 1572872 | tf_op jit(solution)/shard_map/ppermute | solution.py:229
  73.8 0.7 pad_maximum_fusion.4
  74.5 3.2 %collective-permute-done.2 = f16[136,2048]{1,0:T(8,128)(2,1)S(1)} collective-permute-done((f16[136,2048]{1,0:T(8,128)(2,1)S(1)}, f16[136,2048]{1,0:T(8,128)(2,1)S(1)}, u32[]{:S(2)}, u32[]{:S(2)}) %collective-permute-start.2) | collective-permute-done | bytes 557088 | tf_op jit(solution)/shard_map/ppermute | solution.py:229
  77.7 0.5 slice.85
  79.0 0.6 slice.89
  80.3 1.0 abs_reduce_fusion.1
  82.8 1.9 %multiply_convert_fusion.1 = (f16[128,2048]{1,0:T(8,128)(2,1)S(1)}, f16[128,2048]{1,0:T(8,128)(2,1)S(1)}) fusion(f32[512,2048]{1,0:T(8,128)} %forward.1, s32[]{:T(128)S(6)} %select_n.50, f32[]{:T(128)S(6)} %exp2.85, f32[]{:T(128)} %bitcast.4, f16[136,2048]{1,0:T(8,128)(2,1)S(1)} %collective-permute-done.2, f32[]{:T(128)S(6)} %exp2.93, f32[]{:T(128)} %bitcast.7, ...), kind=kLoop, calls=%fused_computation.4 | loop fusion | flops 2621440 | bytes 4194328 | tf_op jit(solution)/shard_map/convert_element_type | solution.py:214
  84.7 0.1 concatenate.31
  84.9 1.3 %collective-permute-start.5 = (f16[136,2048]{1,0:T(8,128)(2,1)S(1)}, f16[136,2048]{1,0:T(8,128)(2,1)S(1)}, u32[]{:S(2)}, u32[]{:S(2)}) collective-permute-start(f16[136,2048]{1,0:T(8,128)(2,1)S(1)} %concatenate.31), channel_id=1, source_target_pairs={{24,16},{16,8},{8,0},{25,17},{17,9},{9,1},{26,18},{18,10},{10,2},{... | collective-permute-start | bytes 1671176 | tf_op jit(solution)/shard_map/ppermute | solution.py:229
  86.2 0.1 concatenate.30
  86.3 2.4 %collective-permute-done.11 = bf16[128,2048]{1,0:T(8,128)(2,1)S(1)} collective-permute-done((bf16[128,2048]{1,0:T(8,128)(2,1)S(1)}, bf16[128,2048]{1,0:T(8,128)(2,1)S(1)}, u32[]{:S(2)}, u32[]{:S(2)}) %collective-permute-start.11) | collective-permute-done | bytes 524320 | tf_op jit(solution)/shard_map/ppermute | solution.py:229
  88.7 5.8 %collective-permute-start.3 = (f16[136,2048]{1,0:T(8,128)(2,1)S(1)}, f16[136,2048]{1,0:T(8,128)(2,1)S(1)}, u32[]{:S(2)}, u32[]{:S(2)}) collective-permute-start(f16[136,2048]{1,0:T(8,128)(2,1)S(1)} %concatenate.30), channel_id=1, source_target_pairs={{0,8},{8,16},{16,24},{1,9},{9,17},{17,25},{2,10},{10,18},{18,26},{... | collective-permute-start | bytes 1671176 | tf_op jit(solution)/shard_map/ppermute | solution.py:229
  94.5 0.1 broadcast_select_fusion.2.refs_3_
  94.6 0.0 copy-start.2
  94.6 0.1 collective-permute-start.12
  94.7 9.9 %backward.2.refs_5_ = f32[128,2048]{1,0:T(8,128)} custom-call(s32[2]{0:T(128)} %get-tuple-element.20.where_ref, bf16[128,1024]{1,0:T(8,128)(2,1)} %collective-permute-done.13.refs_0_, bf16[128,1024]{1,0:T(8,128)(2,1)} %collective-permute-done.14.refs_1_, bf16[128,2048]{1,0:T(8,128)(2,1)} %bitcast.17, bf16[128,2048]{1,0:T(8,128)(2,1)} %copy-done.5, ...), custom_call_target="tpu_custom_call" | custom-call | flops 3623878656 | bytes 4587520 | tf_op jit(solution)/shard_map/backward/pallas_call | solution.py:124
  104.7 0.7 copy-done.11
  105.3 10.0 %backward.3 = bf16[128,2048]{1,0:T(8,128)(2,1)} custom-call(s32[2]{0:T(128)} %get-tuple-element.19.where_ref, bf16[128,1024]{1,0:T(8,128)(2,1)} %collective-permute-done.10.refs_0_, bf16[128,1024]{1,0:T(8,128)(2,1)} %copy-done.11, bf16[128,2048]{1,0:T(8,128)(2,1)} %copy-done.4, bf16[128,2048]{1,0:T(8,128)(2,1)} %copy-done.2, bf16[27,128,512]{2,1,0:T(8,128)(2,1)} %refs_4_.3, ...), custom_call_target="tpu_custom_call" | custom-call | flops 3623878656 | bytes 4587520 | tf_op jit(solution)/shard_map/backward/pallas_call | solution.py:124
  115.3 2.2 %reshape.57 = bf16[128,4,512]{2,1,0:T(4,128)(2,1)} reshape(bf16[128,2048]{1,0:T(8,128)(2,1)} %backward.3) | data formatting | bytes 1048576 | tf_op jit(solution)/shard_map/reshape | solution.py:271
  117.5 0.5 slice.91
  118.7 0.5 slice.87
  120.0 1.5 %add_convert_fusion = bf16[128,2048]{1,0:T(8,128)(2,1)S(1)} fusion(f32[512,2048]{1,0:T(8,128)} %forward.1, s32[]{:T(128)S(6)} %select_n.48, f16[136,2048]{1,0:T(8,128)(2,1)S(1)} %collective-permute-done.5, f16[136,2048]{1,0:T(8,128)(2,1)S(1)} %collective-permute-done.3, f32[]{:T(128)} %bitcast.8, f32[]{:T(128)} %bitcast.5), kind=kLoop, calls=%fused_computation | loop fusion | flops 1835008 | bytes 2621452 | tf_op jit(solution)/shard_map/convert_element_type | solution.py:269
  121.5 1.2 reshape.55
  (41 shorter events, 0.2 us)
Async XLA Ops:
  1.8 2.6 %copy-start.3 = (bf16[16,8,4,512]{3,1,2,0:T(8,128)(2,1)}, bf16[16,8,4,512]{3,1,2,0:T(8,128)(2,1)S(1)}, u32[]{:S(2)}) copy-start(bf16[16,8,4,512]{3,1,2,0:T(8,128)(2,1)S(1)} %copy.12) | copy-start | bytes 1572868
  1.8 2.5 %collective-permute-start = (bf16[128,1024]{1,0:T(8,128)(2,1)S(1)}, bf16[128,1024]{1,0:T(8,128)(2,1)S(1)}, u32[]{:S(2)}, u32[]{:S(2)}) collective-permute-start(bf16[128,1024]{1,0:T(8,128)(2,1)S(1)} %pad_maximum_fusion), channel_id=1, source_target_pairs={{0,4},{4,0},{1,5},{5,1},{2,6},{6,2},{3,7},{7,3},{8,12},{12,8},{9,1... | collective-permute-start | bytes 786440 | tf_op jit(solution)/shard_map/ppermute | solution.py:202
  4.3 24.8 %copy-start.6 = (bf16[128,4,512]{2,1,0:T(4,128)(2,1)S(1)}, bf16[128,4,512]{2,1,0:T(4,128)(2,1)}, u32[]{:S(2)}) copy-start(bf16[128,4,512]{2,1,0:T(4,128)(2,1)} %param.12) | copy-start | bytes 1572868
  4.3 0.7 copy-start.10
  20.4 11.8 %copy-start.16 = (s32[4]{0:T(128)S(1)}, s32[4]{0:T(128)}, u32[]{:S(2)}) copy-start(s32[4]{0:T(128)} %constant.68.clone) | copy-start | bytes 52
  20.4 13.0 %copy-start.15 = (s32[4]{0:T(128)S(1)}, s32[4]{0:T(128)}, u32[]{:S(2)}) copy-start(s32[4]{0:T(128)} %constant.67.clone) | copy-start | bytes 52
  20.4 14.3 %copy-start.14 = (s32[4]{0:T(128)S(1)}, s32[4]{0:T(128)}, u32[]{:S(2)}) copy-start(s32[4]{0:T(128)} %constant.69.clone) | copy-start | bytes 52
  20.4 15.5 %copy-start.13 = (s32[4]{0:T(128)S(1)}, s32[4]{0:T(128)}, u32[]{:S(2)}) copy-start(s32[4]{0:T(128)} %constant.70.clone) | copy-start | bytes 52
  20.4 16.2 %copy-start.12 = (s32[4]{0:T(128)S(1)}, s32[4]{0:T(128)}, u32[]{:S(2)}) copy-start(s32[4]{0:T(128)} %constant.66.clone) | copy-start | bytes 52
  24.5 30.3 %collective-permute-start.1 = (f16[136,2048]{1,0:T(8,128)(2,1)S(1)}, f16[136,2048]{1,0:T(8,128)(2,1)S(1)}, u32[]{:S(2)}, u32[]{:S(2)}) collective-permute-start(f16[136,2048]{1,0:T(8,128)(2,1)S(1)} %concatenate.28), channel_id=1, source_target_pairs={{0,8},{24,16},{1,9},{25,17},{2,10},{26,18},{3,11},{27,19},{4,12},{... | collective-permute-start | bytes 1671176 | tf_op jit(solution)/shard_map/ppermute | solution.py:229
  29.2 42.4 %copy-start.1 = (bf16[16,8,4,512]{3,1,2,0:T(8,128)(2,1)}, bf16[16,8,4,512]{3,1,2,0:T(8,128)(2,1)S(1)}, u32[]{:S(2)}) copy-start(bf16[16,8,4,512]{3,1,2,0:T(8,128)(2,1)S(1)} %copy.13) | copy-start | bytes 1572868
  29.2 23.5 %collective-permute-start.7 = (bf16[128,2048]{1,0:T(8,128)(2,1)S(1)}, bf16[128,2048]{1,0:T(8,128)(2,1)S(1)}, u32[]{:S(2)}, u32[]{:S(2)}) collective-permute-start(bf16[128,2048]{1,0:T(8,128)(2,1)S(1)} %bitcast.14), channel_id=1, source_target_pairs={{0,8},{8,16},{16,24},{1,9},{9,17},{17,25},{2,10},{10,18},{18,26},{... | collective-permute-start | bytes 1572872 | tf_op jit(solution)/shard_map/ppermute | solution.py:229
  30.6 22.9 %collective-permute-start.6 = (bf16[128,2048]{1,0:T(8,128)(2,1)S(1)}, bf16[128,2048]{1,0:T(8,128)(2,1)S(1)}, u32[]{:S(2)}, u32[]{:S(2)}) collective-permute-start(bf16[128,2048]{1,0:T(8,128)(2,1)S(1)} %bitcast.15), channel_id=1, source_target_pairs={{8,0},{16,8},{24,16},{9,1},{17,9},{25,17},{10,2},{18,10},{26,18},{... | collective-permute-start | bytes 1572872 | tf_op jit(solution)/shard_map/ppermute | solution.py:229
  31.9 62.7 %collective-permute-start.13 = (bf16[128,1024]{1,0:T(8,128)(2,1)S(1)}, bf16[128,1024]{1,0:T(8,128)(2,1)}, u32[]{:S(2)}, u32[]{:S(2)}) collective-permute-start(bf16[128,1024]{1,0:T(8,128)(2,1)S(1)} %pad_maximum_fusion.3), channel_id=1, source_target_pairs={{0,4},{4,0},{1,5},{5,1},{2,6},{6,2},{3,7},{7,3},{8,12},{12,8},{9,1... | collective-permute-start | bytes 786440 | tf_op jit(solution)/shard_map/ppermute | solution.py:202
  52.8 14.1 %copy-start.7 = (bf16[128,2048]{1,0:T(8,128)(2,1)}, bf16[128,2048]{1,0:T(8,128)(2,1)S(1)}, u32[]{:S(2)}) copy-start(bf16[128,2048]{1,0:T(8,128)(2,1)S(1)} %collective-permute-done.7) | copy-start | bytes 1572868
  52.8 14.1 %collective-permute-start.8 = (bf16[128,2048]{1,0:T(8,128)(2,1)S(1)}, bf16[128,2048]{1,0:T(8,128)(2,1)S(1)}, u32[]{:S(2)}, u32[]{:S(2)}) collective-permute-start(bf16[128,2048]{1,0:T(8,128)(2,1)S(1)} %collective-permute-done.7), channel_id=1, source_target_pairs={{8,16},{16,24},{9,17},{17,25},{10,18},{18,26},{11,19},{19,27},{12,... | collective-permute-start | bytes 1572872 | tf_op jit(solution)/shard_map/ppermute | solution.py:229
  53.5 13.4 %copy-start.8 = (bf16[128,2048]{1,0:T(8,128)(2,1)}, bf16[128,2048]{1,0:T(8,128)(2,1)S(1)}, u32[]{:S(2)}) copy-start(bf16[128,2048]{1,0:T(8,128)(2,1)S(1)} %collective-permute-done.6) | copy-start | bytes 1572868
  53.5 16.8 %collective-permute-start.9 = (bf16[128,2048]{1,0:T(8,128)(2,1)S(1)}, bf16[128,2048]{1,0:T(8,128)(2,1)}, u32[]{:S(2)}, u32[]{:S(2)}) collective-permute-start(bf16[128,2048]{1,0:T(8,128)(2,1)S(1)} %collective-permute-done.6), channel_id=1, source_target_pairs={{16,8},{8,0},{17,9},{9,1},{18,10},{10,2},{19,11},{11,3},{20,12},{1... | collective-permute-start | bytes 1572872 | tf_op jit(solution)/shard_map/ppermute | solution.py:229
  58.8 21.5 %copy-start = (f32[512,2048]{1,0:T(8,128)S(1)}, f32[512,2048]{1,0:T(8,128)}, u32[]{:S(2)}) copy-start(f32[512,2048]{1,0:T(8,128)} %forward.1) | copy-start | bytes 12582916
  60.5 17.3 %collective-permute-start.2 = (f16[136,2048]{1,0:T(8,128)(2,1)S(1)}, f16[136,2048]{1,0:T(8,128)(2,1)S(1)}, u32[]{:S(2)}, u32[]{:S(2)}) collective-permute-start(f16[136,2048]{1,0:T(8,128)(2,1)S(1)} %concatenate.29), channel_id=1, source_target_pairs={{0,8},{8,16},{1,9},{9,17},{2,10},{10,18},{3,11},{11,19},{4,12},{12... | collective-permute-start | bytes 1671176 | tf_op jit(solution)/shard_map/ppermute | solution.py:229
  66.2 12.8 %collective-permute-start.4 = (f16[136,2048]{1,0:T(8,128)(2,1)S(1)}, f16[136,2048]{1,0:T(8,128)(2,1)S(1)}, u32[]{:S(2)}, u32[]{:S(2)}) collective-permute-start(f16[136,2048]{1,0:T(8,128)(2,1)S(1)} %concatenate.29), channel_id=1, source_target_pairs={{24,16},{16,8},{25,17},{17,9},{26,18},{18,10},{27,19},{19,11},{28,... | collective-permute-start | bytes 1671176 | tf_op jit(solution)/shard_map/ppermute | solution.py:229
  66.9 0.8 copy-start.9
  71.6 13.1 %copy-start.4 = (bf16[128,2048]{1,0:T(8,128)(2,1)}, bf16[128,2048]{1,0:T(8,128)(2,1)S(1)}, u32[]{:S(2)}) copy-start(bf16[128,2048]{1,0:T(8,128)(2,1)S(1)} %get-tuple-element.4.refs_2_) | copy-start | bytes 1572868
  71.6 13.1 %copy-start.5 = (bf16[128,2048]{1,0:T(8,128)(2,1)}, bf16[128,2048]{1,0:T(8,128)(2,1)S(1)}, u32[]{:S(2)}) copy-start(bf16[128,2048]{1,0:T(8,128)(2,1)S(1)} %get-tuple-element.10.refs_3_) | copy-start | bytes 1572868
  72.5 32.1 %collective-permute-start.10 = (bf16[128,1024]{1,0:T(8,128)(2,1)}, bf16[128,1024]{1,0:T(8,128)(2,1)}, u32[]{:S(2)}, u32[]{:S(2)}) collective-permute-start(bf16[128,1024]{1,0:T(8,128)(2,1)} %pad_maximum_fusion.1), channel_id=1, source_target_pairs={{0,4},{4,0},{1,5},{5,1},{2,6},{6,2},{3,7},{7,3},{8,12},{12,8},{9,1... | collective-permute-start | bytes 786440 | tf_op jit(solution)/shard_map/ppermute | solution.py:202
  72.5 16.2 %collective-permute-start.11 = (bf16[128,2048]{1,0:T(8,128)(2,1)S(1)}, bf16[128,2048]{1,0:T(8,128)(2,1)S(1)}, u32[]{:S(2)}, u32[]{:S(2)}) collective-permute-start(bf16[128,2048]{1,0:T(8,128)(2,1)S(1)} %get-tuple-element.5), channel_id=1, source_target_pairs={{16,24},{8,0},{17,25},{9,1},{18,26},{10,2},{19,27},{11,3},{20,28},... | collective-permute-start | bytes 1572872 | tf_op jit(solution)/shard_map/ppermute | solution.py:229
  77.7 17.0 %collective-permute-start.14 = (bf16[128,1024]{1,0:T(8,128)(2,1)}, bf16[128,1024]{1,0:T(8,128)(2,1)}, u32[]{:S(2)}, u32[]{:S(2)}) collective-permute-start(bf16[128,1024]{1,0:T(8,128)(2,1)} %pad_maximum_fusion.4), channel_id=1, source_target_pairs={{0,4},{4,0},{1,5},{5,1},{2,6},{6,2},{3,7},{7,3},{8,12},{12,8},{9,1... | collective-permute-start | bytes 786440 | tf_op jit(solution)/shard_map/ppermute | solution.py:202
  84.9 32.7 %collective-permute-start.5 = (f16[136,2048]{1,0:T(8,128)(2,1)S(1)}, f16[136,2048]{1,0:T(8,128)(2,1)S(1)}, u32[]{:S(2)}, u32[]{:S(2)}) collective-permute-start(f16[136,2048]{1,0:T(8,128)(2,1)S(1)} %concatenate.31), channel_id=1, source_target_pairs={{24,16},{16,8},{8,0},{25,17},{17,9},{9,1},{26,18},{18,10},{10,2},{... | collective-permute-start | bytes 1671176 | tf_op jit(solution)/shard_map/ppermute | solution.py:229
  88.7 30.0 %collective-permute-start.3 = (f16[136,2048]{1,0:T(8,128)(2,1)S(1)}, f16[136,2048]{1,0:T(8,128)(2,1)S(1)}, u32[]{:S(2)}, u32[]{:S(2)}) collective-permute-start(f16[136,2048]{1,0:T(8,128)(2,1)S(1)} %concatenate.30), channel_id=1, source_target_pairs={{0,8},{8,16},{16,24},{1,9},{9,17},{17,25},{2,10},{10,18},{18,26},{... | collective-permute-start | bytes 1671176 | tf_op jit(solution)/shard_map/ppermute | solution.py:229
  94.6 10.1 %copy-start.2 = (bf16[128,2048]{1,0:T(8,128)(2,1)}, bf16[128,2048]{1,0:T(8,128)(2,1)S(1)}, u32[]{:S(2)}) copy-start(bf16[128,2048]{1,0:T(8,128)(2,1)S(1)} %broadcast_select_fusion.2.refs_3_) | copy-start | bytes 1572868
  94.6 10.0 %collective-permute-start.12 = (bf16[128,1024]{1,0:T(8,128)(2,1)S(1)}, bf16[128,1024]{1,0:T(8,128)(2,1)S(1)}, u32[]{:S(2)}, u32[]{:S(2)}) collective-permute-start(bf16[128,1024]{1,0:T(8,128)(2,1)S(1)} %pad_maximum_fusion.2), channel_id=1, source_target_pairs={{0,4},{4,0},{1,5},{5,1},{2,6},{6,2},{3,7},{7,3},{8,12},{12,8},{9,1... | collective-permute-start | bytes 786440 | tf_op jit(solution)/shard_map/ppermute | solution.py:202
  104.6 0.7 copy-start.11
where the time goes:
time: 123 us
  Pallas kernels  35.2 us (29%)
  starting transfers between devices  24.7 us (20%)
  waiting for transfers between devices  21.4 us (17%)
  other arithmetic  16.7 us (14%)
  local copies, waits for them, and re-layouts  14.4 us (12%)
  between operations  10.2 us (8%)
    ppermute x10, starting transfers between devices, line_of_four(): move = lambda a, pairs: lax.ppermute(a, 'chan', pairs)  23.9 us
    ppermute x10, waiting for transfers between devices, line_of_four(): move = lambda a, pairs: lax.ppermute(a, 'chan', pairs)  21.4 us
    pallas_call x2, Pallas kernels, backward(): pl.pallas_call(functools.partial(backward_kernel, slab, number, first), g...  19.9 us
    pallas_call x1, Pallas kernels, forward(): pl.pallas_call(functools.partial(forward_kernel, slab), grid=(slab,), in_...  15.3 us
    reduce_max x3, other arithmetic, pack(): top = jnp.max(jnp.abs(total))  4.98 us
    convert_element_type x3, other arithmetic, pack(): scaled = (total * jnp.exp2(15.0 - power)).astype(jnp.float16)  4.85 us
    dynamic_slice x6, local copies, waits for them, and re-layouts, line_of_four(): pick = lambda *options: jnp.asarray(options, jnp.int32)[place]  4.29 us
    unnamed x36, local copies, waits for them, and re-layouts  3.49 us
  transfers between devices with their start and end apart: 15, of which 4 were waited for; matrix products, arithmetic and copies ran while one was open for 17% of the time, Pallas kernels for 16%

commit v1 on v0

--- a/solution.py
+++ b/solution.py
@@ -7,9 +7,11 @@
 from jax.experimental.pallas import tpu as pltpu
 from jax.sharding import PartitionSpec as P
 
+
 NZ = 64
 OFFSETS = (-1, 0, 1)
 VMEM_LIMIT = 56 * 2**20
+
 
 def shift_z(block, offset):
     if offset == 0:
@@ -21,12 +23,14 @@
     edge = z == (0 if offset == 1 else NZ - 1)
     return jnp.where(edge, wrapped, plain)
 
+
 def shift_y(block, offset):
     if offset == 0:
         return block
     return pltpu.roll(block, (NZ * offset) % block.shape[1], 1)
 
-def forward_kernel(slab, halo_ref, x_ref, w_ref, out_ref, columns, wt):
+
+def forward_kernel(slab, position_ref, halo_ref, x_ref, w_ref, out_ref, marks_ref, columns, wt, top_ref):
     plane = pl.program_id(0)
     chans, size = w_ref.shape[1], out_ref.shape[1]
 
@@ -54,26 +58,64 @@
                        preferred_element_type=jnp.float32)
         total = part if total is None else total + part
     out_ref[...] = total
-
-def forward(x, halo, w, slab):
+    top = jnp.max(jnp.max(jnp.abs(total), axis=0, keepdims=True), axis=1, keepdims=True)
+    top = jnp.broadcast_to(top, top_ref.shape)
+
+    @pl.when(plane == 0)
+    def _():
+        top_ref[...] = top
+
+    @pl.when(plane > 0)
+    def _():
+        top_ref[...] = jnp.maximum(top_ref[...], top)
+
+    @pl.when(plane == slab - 1)
+    def _():
+        power = jnp.clip(jnp.ceil(jnp.log2(jnp.maximum(top_ref[...], 1e-30))), -28.0, 15.0)
+        high = jnp.maximum(power, -14.0)
+        row = lax.broadcasted_iota(jnp.int32, top_ref.shape, 0) - 2 * position_ref[0]
+        mark = jnp.where(row == 0, jnp.exp2(high), jnp.where(row == 1, jnp.exp2(power - high), 0.0))
+        for lane in range(0, marks_ref.shape[1], mark.shape[1]):
+            marks_ref[:, lane : lane + mark.shape[1]] = mark
+
+
+def forward(position, x, halo, w, slab):
     chans, cells = x.shape
     size = cells // slab
     full = w.shape[2]
-    whole = lambda a: pl.BlockSpec(a.shape, lambda n: (0,) * a.ndim, pipeline_mode=pl.Buffered(1))
+    whole = lambda a: pl.BlockSpec(a.shape, lambda n, s: (0,) * a.ndim, pipeline_mode=pl.Buffered(1))
     return pl.pallas_call(
         functools.partial(forward_kernel, slab),
-        grid=(slab,),
-        in_specs=[whole(halo), whole(x), whole(w)],
-        out_specs=pl.BlockSpec((full, size), lambda n: (0, n)),
-        out_shape=jax.ShapeDtypeStruct((full, cells), jnp.float32),
-        scratch_shapes=[pltpu.VMEM((9 * chans, (slab + 2) * size), jnp.bfloat16),
-                        pltpu.VMEM((full, 27 * chans), jnp.bfloat16)],
+        grid_spec=pltpu.PrefetchScalarGridSpec(
+            num_scalar_prefetch=1,
+            grid=(slab,),
+            in_specs=[whole(halo), whole(x), whole(w)],
+            out_specs=[
+                pl.BlockSpec((full, size), lambda n, s: (0, n)),
+                pl.BlockSpec((8, cells), lambda n, s: (0, 0)),
+            ],
+            scratch_shapes=[
+                pltpu.VMEM((9 * chans, (slab + 2) * size), jnp.bfloat16),
+                pltpu.VMEM((full, 27 * chans), jnp.bfloat16),
+                pltpu.VMEM((8, 128), jnp.float32),
+            ],
+        ),
+        out_shape=[
+            jax.ShapeDtypeStruct((full, cells), jnp.float32),
+            jax.ShapeDtypeStruct((8, cells), jnp.float32),
+        ],
         compiler_params=pltpu.CompilerParams(vmem_limit_bytes=VMEM_LIMIT),
-        cost_estimate=pl.CostEstimate(flops=2*27*chans*full*cells, bytes_accessed=w.size*2+full*cells*4, transcendentals=0),
+        cost_estimate=pl.CostEstimate(
+            flops=2 * 27 * chans * full * cells,
+            bytes_accessed=w.size * 2 + full * cells * 4,
+            transcendentals=0,
+        ),
         name="forward",
-    )(halo, x, w)
-
-def backward_kernel(slab, number, first, where_ref, *refs):
+    )(position, halo, x, w)
+
+
+def backward_kernel(slab, sources, first, position_ref, *refs):
+    number = len(sources)
     halos, blocks = refs[:number], refs[number:2 * number]
     w_ref = refs[2 * number]
     before = None if first else refs[2 * number + 1]
@@ -85,7 +127,7 @@
     @pl.when(plane == 0)
     def _():
         for k in range(number):
-            at = pl.multiple_of(where_ref[k] * chans, chans)
+            at = pl.multiple_of(sources[k](position_ref[0]) * chans, chans)
             for ix, offset_x in enumerate(OFFSETS):
                 row = (3 * k + ix) * chans
                 for o in range(9):
@@ -112,7 +154,8 @@
         total = over_y if total is None else total + over_y
     out_ref[...] = total.astype(out_ref.dtype)
 
-def backward(where, blocks, halos, w, before, slab, out_dtype):
+
+def backward(position, sources, blocks, halos, w, before, slab, out_dtype):
     number = len(blocks)
     chans, cells = blocks[0].shape
     chans_in = w.shape[1]
@@ -122,7 +165,7 @@
     each = pl.BlockSpec((chans_in, size), lambda n, s: (0, n))
     args = (*halos, *blocks, w) + (() if first else (before,))
     return pl.pallas_call(
-        functools.partial(backward_kernel, slab, number, first),
+        functools.partial(backward_kernel, slab, sources, first),
         grid_spec=pltpu.PrefetchScalarGridSpec(
             num_scalar_prefetch=1, grid=(slab,),
             in_specs=[whole(a) for a in args[:2 * number + 1]] + ([] if first else [each]),
@@ -133,7 +176,7 @@
         compiler_params=pltpu.CompilerParams(vmem_limit_bytes=VMEM_LIMIT),
         cost_estimate=pl.CostEstimate(flops=2*27*chans*chans_in*cells*number, bytes_accessed=w.size*2+chans_in*cells*4, transcendentals=0),
         name="backward",
-    )(where, *args)
+    )(position, *args)
 
 
 def padded(block, sides, width):
@@ -205,30 +248,39 @@
     return jnp.concatenate([low, high], axis=1)
 
 
-MARK_ROWS = 8
-
-
-def pack(total):
-    top = jnp.max(jnp.abs(total))
-    power = jnp.clip(jnp.ceil(jnp.log2(jnp.maximum(top, 1e-36))), -100.0, 100.0)
-    scaled = (total * jnp.exp2(15.0 - power)).astype(jnp.float16)
-    mark = jnp.full((MARK_ROWS, total.shape[1]), power, jnp.float16)
-    return jnp.concatenate([scaled, mark], axis=0)
+LINE = 4
+TOP = 32768.0
+
+
+def scale_of(marks):
+    marks = marks.astype(jnp.float32)
+    return sum(marks[2 * i : 2 * i + 1] * marks[2 * i + 1 : 2 * i + 2] for i in range(LINE))
+
+
+def pack(total, marks):
+    scaled = (total * (TOP / scale_of(marks))).astype(jnp.float16)
+    return jnp.concatenate([scaled, marks], axis=0)
 
 
 def unpack(parcel):
-    rows = parcel.shape[0] - MARK_ROWS
-    power = parcel[rows, 0].astype(jnp.float32)
-    return parcel[:rows].astype(jnp.float32) * jnp.exp2(power - 15.0)
+    rows = parcel.shape[0] - 2 * LINE
+    return parcel[:rows].astype(jnp.float32) * (scale_of(parcel[rows:]) * (1.0 / TOP)), parcel[rows:]
+
+
+def pack_sum(total, marks, parcel):
+    other, other_marks = unpack(parcel)
+    return pack(total + other, marks + other_marks)
 
 
 def line_of_four(inputs, weights, out_grad):
     chans, slab_len, size = inputs.shape
     cells = slab_len * size
     place = lax.axis_index("chan")
-    move = lambda a, pairs: lax.ppermute(a, "chan", pairs)
-    pick = lambda *options: jnp.asarray(options, jnp.int32)[place]
+    position = place.reshape(1)
     middle = (place == 1) | (place == 2)
+
+    def move(block, pairs):
+        return lax.ppermute(block, "chan", pairs)
 
     grad = out_grad.reshape(chans, cells)
     field = inputs.reshape(chans, cells)
@@ -237,22 +289,26 @@
     field_edges = edge_planes(field, size)
     grad_edges = edge_planes(grad, size)
 
-    partial = forward(field, field_edges, weights, slab_len)
+    partial, marks = forward(position, field, field_edges, weights, slab_len)
+    marks = marks.astype(jnp.float16)
     block = lambda index: lax.dynamic_slice_in_dim(partial, index * chans, chans, axis=0)
 
-    sum_1 = move(pack(block(pick(3, 3, 0, 0))), [(0, 1), (3, 2)])
+    sum_1 = move(pack(block(jnp.where(place < 2, 3, 0)), marks), [(0, 1), (3, 2)])
     below_2 = move(from_below, [(1, 2), (2, 3)])
     above_2 = move(from_above, [(2, 1), (1, 0)])
     second = jnp.where(place == 0, from_above, from_below)
     second_edges = edge_planes(second, size)
     grad_half = backward(
-        jnp.stack([place, pick(1, 0, 1, 2)]), (grad, second), (grad_edges, second_edges),
+        position, (own_place, second_place), (grad, second), (grad_edges, second_edges),
         weights, None, slab_len, jnp.float32,
     )
 
-    parcel = pack(block(pick(2, 3, 0, 1)) + unpack(sum_1))
+    parcel = pack_sum(block((place + 2) % 4), marks, sum_1)
     sum_below = move(parcel, [(0, 1), (1, 2)])
     sum_above = move(parcel, [(3, 2), (2, 1)])
+    from_above, below_2, above_2, grad_half = lax.optimization_barrier(
+        (from_above, below_2, above_2, grad_half)
+    )
     relayed = jnp.where(place >= 2, below_2, above_2)
     far = move(relayed, [(2, 3), (1, 0)])
     third = jnp.where(middle, from_above, relayed)
@@ -260,18 +316,36 @@
     third_edges = edge_planes(third, size)
     fourth_edges = edge_planes(fourth, size)
 
-    last_below = move(pack(block(pick(1, 2, 3, 3)) + unpack(sum_below)), [(0, 1), (1, 2), (2, 3)])
-    last_above = move(pack(block(pick(0, 0, 1, 2)) + unpack(sum_above)), [(3, 2), (2, 1), (1, 0)])
+    upward = pack_sum(block(jnp.minimum(place + 1, 3)), marks, sum_below)
+    downward = pack_sum(block(jnp.maximum(place - 1, 0)), marks, sum_above)
+    last_below = move(upward, [(0, 1), (1, 2), (2, 3)])
+    last_above = move(downward, [(3, 2), (2, 1), (1, 0)])
     input_grad = backward(
-        jnp.stack([pick(2, 2, 3, 1), pick(3, 3, 0, 0)]), (third, fourth), (third_edges, fourth_edges),
+        position, (third_place, fourth_place), (third, fourth), (third_edges, fourth_edges),
         weights, grad_half, slab_len, jnp.bfloat16,
     )
-    conv_out = (block(place) + unpack(last_below) + unpack(last_above)).astype(jnp.bfloat16)
+    conv_out = block(place) + unpack(last_below)[0] + unpack(last_above)[0]
     shape = (chans, slab_len, size)
-    return conv_out.reshape(shape), input_grad.reshape(shape)
-
-
-def per_device(inputs, weights, out_grad):
+    return conv_out.astype(jnp.bfloat16).reshape(shape), input_grad.reshape(shape)
+
+
+def own_place(place):
+    return place
+
+
+def second_place(place):
+    return jnp.where(place == 0, 1, place - 1)
+
+
+def third_place(place):
+    return jnp.where(place == 3, 1, jnp.where(place == 2, 3, 2))
+
+
+def fourth_place(place):
+    return jnp.where(place < 2, 3, 0)
+
+
+def chosen(inputs, weights, out_grad):
     chans, size = inputs.shape[0], inputs.shape[2]
     line = lax.axis_size("chan") == 4 and weights.shape[2] == 4 * chans and out_grad.shape[0] == chans
     if line and chans % 128 == 0 and size % 128 == 0:
@@ -286,6 +360,4 @@
         P(("batch", "chan"), "slab", None),
     )
     out_specs = (P(("batch", "chan"), "slab", None), P(("batch", "chan"), "slab", None))
-    return jax.shard_map(
-        per_device, mesh=mesh, in_specs=in_specs, out_specs=out_specs, check_vma=False
-    )
+    return jax.shard_map(chosen, mesh=mesh, in_specs=in_specs, out_specs=out_specs, check_vma=False)

time: 123 us -> 94.2 us (0.77)
  other arithmetic: 16.7 us -> 5.7 us
  between operations: 10.2 us -> 1.16 us
  waiting for transfers between devices: 21.4 us -> 15.5 us
  local copies, waits for them, and re-layouts: 14.4 us -> 8.6 us
  starting transfers between devices: 24.7 us -> 28.4 us
    ppermute x10, waiting for transfers between devices: 21.4 us -> 14.6 us  [move(): return lax.ppermute(block, 'chan', pairs)]
    reduce_max x3 -> x0, other arithmetic: 4.98 us -> none  [pack(): top = jnp.max(jnp.abs(total))]
    dynamic_slice x6 -> x0, local copies, waits for them, and re-layouts: 4.29 us -> none  [line_of_four(): pick = lambda *options: jnp.asarray(options, jnp.int32)[place]]
    ppermute x10, starting transfers between devices: 23.9 us -> 27.4 us  [move(): return lax.ppermute(block, 'chan', pairs)]
    slice x5 -> x0, local copies, waits for them, and re-layouts: 2.68 us -> none  [unpack(): power = parcel[rows, 0].astype(jnp.float32)]
    another operation x1 -> x0, other arithmetic: 2.44 us -> none  [line_of_four(): jnp.stack([pick(2, 2, 3, 1), pick(3, 3, 0, 0)])]
    convert_element_type x4 -> x9, other arithmetic: 6.32 us -> 4.36 us  [the longest x3 1.98 us: pack(): scaled = (total * (TOP / scale_of(marks))).astype(jnp.float16)]
    unnamed x36 -> x22, local copies, waits for them, and re-layouts: 3.49 us -> 5.11 us
  transfers between devices with their start and end apart: 15 -> 15, of which waited for: 4 -> 4; matrix products, arithmetic and copies ran while one was open for 17% -> 8% of each run, Pallas kernels for 16% -> 37%
where the time goes in v1:
time: 94.2 us; the launch traced here: 93.5 us
  Pallas kernels  34.2 us (36%)
  starting transfers between devices  28.4 us (30%)
  waiting for transfers between devices  15.5 us (16%)
  local copies, waits for them, and re-layouts  8.6 us (9%)
  other arithmetic  5.7 us (6%)
  between operations  1.16 us (1%)
    ppermute x10, starting transfers between devices, move(): return lax.ppermute(block, 'chan', pairs)  27.4 us
    pallas_call x2, Pallas kernels, backward(): pl.pallas_call(functools.partial(backward_kernel, slab, sources, first),...  18.5 us
    pallas_call x1, Pallas kernels, forward(): pl.pallas_call(functools.partial(forward_kernel, slab), grid_spec=pltpu.P...  15.7 us
    ppermute x10, waiting for transfers between devices, move(): return lax.ppermute(block, 'chan', pairs)  14.6 us
    unnamed x22, local copies, waits for them, and re-layouts  5.11 us
    reshape x1, local copies, waits for them, and re-layouts, line_of_four(): input_grad.reshape(shape)  2.22 us
    convert_element_type x3, other arithmetic, pack(): scaled = (total * (TOP / scale_of(marks))).astype(jnp.float16)  1.98 us
  transfers between devices with their start and end apart: 15, of which 4 were waited for; matrix products, arithmetic and copies ran while one was open for 8% of the time, Pallas kernels for 37%

profile of v1, /device:TPU:0, one launch (start us, length us, event | category | flops | bytes accessed | tf_op | source)
XLA Modules:
  0.0 93.5 jit_solution(719926681457273212)
XLA Ops:
  0.6 1.1 %copy.6 = bf16[16,8,4,512]{3,1,2,0:T(8,128)(2,1)S(1)} copy(bf16[16,8,4,512]{3,2,1,0:T(4,128)(2,1)} %bitcast.20) | data formatting | bytes 1048576
  1.8 0.0 copy-start.2
  1.8 1.3 %collective-permute-start.6 = (bf16[128,2048]{1,0:T(8,128)(2,1)S(1)}, bf16[128,2048]{1,0:T(8,128)(2,1)S(1)}, u32[]{:S(2)}, u32[]{:S(2)}) collective-permute-start(bf16[128,2048]{1,0:T(8,128)(2,1)S(1)} %bitcast.14), channel_id=1, source_target_pairs={{8,0},{16,8},{24,16},{9,1},{17,9},{25,17},{10,2},{18,10},{26,18},{... | collective-permute-start | bytes 1572872 | tf_op jit(solution)/shard_map/ppermute | solution.py:283
  3.1 6.4 %collective-permute-start.7 = (bf16[128,2048]{1,0:T(8,128)(2,1)S(1)}, bf16[128,2048]{1,0:T(8,128)(2,1)}, u32[]{:S(2)}, u32[]{:S(2)}) collective-permute-start(bf16[128,2048]{1,0:T(8,128)(2,1)S(1)} %bitcast.15), channel_id=1, source_target_pairs={{0,8},{8,16},{16,24},{1,9},{9,17},{17,25},{2,10},{10,18},{18,26},{... | collective-permute-start | bytes 1572872 | tf_op jit(solution)/shard_map/ppermute | solution.py:283
  9.5 1.1 %copy.5 = bf16[16,8,4,512]{3,1,2,0:T(8,128)(2,1)S(1)} copy(bf16[16,8,4,512]{3,2,1,0:T(4,128)(2,1)} %bitcast.21) | data formatting | bytes 1048576
  10.6 0.0 copy-start.4
  10.7 0.1 collective-permute-start
  10.8 0.6 collective-permute-start.10
  11.4 0.9 collective-permute-done.halo_ref
  12.3 0.7 copy-done.8
  13.0 15.7 %forward.1 = (f32[512,2048]{1,0:T(8,128)}, f32[8,2048]{1,0:T(8,128)}) custom-call(s32[1]{0:T(128)} %bitcast.position_ref, bf16[128,1024]{1,0:T(8,128)(2,1)} %copy-done.8, bf16[128,2048]{1,0:T(8,128)(2,1)} %bitcast.19, bf16[27,128,512]{2,1,0:T(8,128)(2,1)} %refs_4_.3), custom_call_target="tpu_custom_call" | custom-call | flops 7247757312 | bytes 7733248 | tf_op jit(solution)/shard_map/forward/pallas_call | solution.py:87
  28.7 0.8 fusion.39
  29.6 0.1 fusion.27
  29.6 1.3 %multiply_convert_fusion.3 = f16[128,2048]{1,0:T(8,128)(2,1)S(1)} fusion(f32[512,2048]{1,0:T(8,128)} %get-tuple-element.8, s32[]{:T(128)S(6)} %select_n.55, f32[2048]{0:T(1024)S(1)} %bitcast.30), kind=kLoop, calls=%fused_computation.4 | loop fusion | flops 524288 | bytes 1581060 | tf_op jit(solution)/shard_map/convert_element_type | solution.py:261
  31.0 0.0 collective-permute-done.6
  31.0 0.0 collective-permute-done.7
  31.0 0.1 broadcast_select_fusion.1.refs_3_
  31.0 0.0 copy-start.3
  31.1 0.2 collective-permute-start.11
  31.3 0.1 pad_maximum_fusion
  31.4 4.2 %collective-permute-start.1 = (f16[136,2048]{1,0:T(8,128)(2,1)S(1)}, f16[136,2048]{1,0:T(8,128)(2,1)S(1)}, u32[]{:S(2)}, u32[]{:S(2)}) collective-permute-start(f16[136,2048]{1,0:T(8,128)(2,1)S(1)} %pad_maximum_fusion), channel_id=1, source_target_pairs={{0,8},{24,16},{1,9},{25,17},{2,10},{26,18},{3,11},{27,19},{4,12},{... | collective-permute-start | bytes 1671176 | tf_op jit(solution)/shard_map/ppermute | solution.py:283
  35.7 0.8 collective-permute-start.8
  36.5 1.4 %collective-permute-start.9 = (bf16[128,2048]{1,0:T(8,128)(2,1)S(1)}, bf16[128,2048]{1,0:T(8,128)(2,1)S(1)}, u32[]{:S(2)}, u32[]{:S(2)}) collective-permute-start(bf16[128,2048]{1,0:T(8,128)(2,1)S(1)} %collective-permute-done.6), channel_id=1, source_target_pairs={{16,8},{8,0},{17,9},{9,1},{18,10},{10,2},{19,11},{11,3},{20,12},{1... | collective-permute-start | bytes 1572872 | tf_op jit(solution)/shard_map/ppermute | solution.py:283
  38.0 0.0 collective-permute-done.10.refs_0_
  38.0 0.0 collective-permute-done.11.refs_1_
  38.0 0.7 copy-done.6
  38.7 9.2 %backward.2.refs_5_ = f32[128,2048]{1,0:T(8,128)} custom-call(s32[1]{0:T(128)} %bitcast.position_ref, bf16[128,1024]{1,0:T(8,128)(2,1)} %copy-done.6, bf16[128,1024]{1,0:T(8,128)(2,1)} %collective-permute-done.11.refs_1_, bf16[128,2048]{1,0:T(8,128)(2,1)} %bitcast.17, bf16[128,2048]{1,0:T(8,128)(2,1)} %copy-done.3, bf16[27,128,512]{2,1,0:T(8,128)(2,1)} %refs_4_.3), custom_call_target="tpu_custom_call" | custom-call | flops 3623878656 | bytes 4587520 | tf_op jit(solution)/shard_map/backward/pallas_call | solution.py:167
  47.9 0.1 collective-permute-done.1
  48.0 0.1 fusion.28
  48.2 0.2 multiply_convert_fusion.2
  48.4 0.1 pad_maximum_fusion.1
  48.5 0.7 collective-permute-start.4
  49.2 5.2 %collective-permute-start.2 = (f16[136,2048]{1,0:T(8,128)(2,1)S(1)}, f16[136,2048]{1,0:T(8,128)(2,1)S(1)}, u32[]{:S(2)}, u32[]{:S(2)}) collective-permute-start(f16[136,2048]{1,0:T(8,128)(2,1)S(1)} %pad_maximum_fusion.1), channel_id=1, source_target_pairs={{0,8},{8,16},{1,9},{9,17},{2,10},{10,18},{3,11},{11,19},{4,12},{12... | collective-permute-start | bytes 1671176 | tf_op jit(solution)/shard_map/ppermute | solution.py:283
  54.4 0.0 collective-permute-done.8
  54.5 0.1 broadcast_select_fusion.3
  54.6 0.0 copy-start.1
  54.6 0.1 collective-permute-start.12
  54.7 1.3 %collective-permute-start.13 = (bf16[128,2048]{1,0:T(8,128)(2,1)S(1)}, bf16[128,2048]{1,0:T(8,128)(2,1)S(1)}, u32[]{:S(2)}, u32[]{:S(2)}) collective-permute-start(bf16[128,2048]{1,0:T(8,128)(2,1)S(1)} %get-tuple-element.15), channel_id=1, source_target_pairs={{16,24},{8,0},{17,25},{9,1},{18,26},{10,2},{19,27},{11,3},{20,28},... | collective-permute-start | bytes 1572872 | tf_op jit(solution)/shard_map/ppermute | solution.py:283
  56.0 0.0 collective-permute-done.4
  56.0 10.5 %collective-permute-done.2 = f16[136,2048]{1,0:T(8,128)(2,1)S(1)} collective-permute-done((f16[136,2048]{1,0:T(8,128)(2,1)S(1)}, f16[136,2048]{1,0:T(8,128)(2,1)S(1)}, u32[]{:S(2)}, u32[]{:S(2)}) %collective-permute-start.2) | collective-permute-done | bytes 557088 | tf_op jit(solution)/shard_map/ppermute | solution.py:283
  66.6 0.1 fusion.31
  66.6 0.1 fusion.30
  66.7 0.1 fusion.34
  66.8 0.1 fusion.33
  66.8 0.5 multiply_convert_fusion.1
  67.3 3.9 %collective-permute-done.13 = bf16[128,2048]{1,0:T(8,128)(2,1)S(1)} collective-permute-done((bf16[128,2048]{1,0:T(8,128)(2,1)S(1)}, bf16[128,2048]{1,0:T(8,128)(2,1)S(1)}, u32[]{:S(2)}, u32[]{:S(2)}) %collective-permute-start.13) | collective-permute-done | bytes 524320 | tf_op jit(solution)/shard_map/ppermute | solution.py:283
  71.2 0.1 broadcast_select_fusion.2.refs_3_
  71.3 0.0 copy-start.5
  71.3 0.1 collective-permute-start.14
  71.4 0.1 pad_maximum_fusion.3
  71.6 1.3 %collective-permute-start.5 = (f16[136,2048]{1,0:T(8,128)(2,1)S(1)}, f16[136,2048]{1,0:T(8,128)(2,1)S(1)}, u32[]{:S(2)}, u32[]{:S(2)}) collective-permute-start(f16[136,2048]{1,0:T(8,128)(2,1)S(1)} %pad_maximum_fusion.3), channel_id=1, source_target_pairs={{24,16},{16,8},{8,0},{25,17},{17,9},{9,1},{26,18},{18,10},{10,2},{... | collective-permute-start | bytes 1671176 | tf_op jit(solution)/shard_map/ppermute | solution.py:283
  72.9 0.1 pad_maximum_fusion.2
  73.0 4.8 %collective-permute-start.3 = (f16[136,2048]{1,0:T(8,128)(2,1)S(1)}, f16[136,2048]{1,0:T(8,128)(2,1)S(1)}, u32[]{:S(2)}, u32[]{:S(2)}) collective-permute-start(f16[136,2048]{1,0:T(8,128)(2,1)S(1)} %pad_maximum_fusion.2), channel_id=1, source_target_pairs={{0,8},{8,16},{16,24},{1,9},{9,17},{17,25},{2,10},{10,18},{18,26},{... | collective-permute-start | bytes 1671176 | tf_op jit(solution)/shard_map/ppermute | solution.py:283
  77.8 0.0 collective-permute-done.12.refs_0_
  77.8 0.0 collective-permute-done.14.refs_1_
  77.8 0.7 copy-done.7
  78.5 0.7 copy-done.9
  79.2 9.3 %backward.3 = bf16[128,2048]{1,0:T(8,128)(2,1)} custom-call(s32[1]{0:T(128)} %bitcast.position_ref, bf16[128,1024]{1,0:T(8,128)(2,1)} %copy-done.7, bf16[128,1024]{1,0:T(8,128)(2,1)} %copy-done.9, bf16[128,2048]{1,0:T(8,128)(2,1)} %copy-done.1, bf16[128,2048]{1,0:T(8,128)(2,1)} %copy-done.5, bf16[27,128,512]{2,1,0:T(8,128)(2,1)} %refs_4_.3, ...), custom_call_target="tpu_custom_call" | custom-call | flops 3623878656 | bytes 4587520 | tf_op jit(solution)/shard_map/backward/pallas_call | solution.py:167
  88.5 2.2 %reshape.23 = bf16[128,4,512]{2,1,0:T(4,128)(2,1)} reshape(bf16[128,2048]{1,0:T(8,128)(2,1)} %backward.3) | data formatting | bytes 1048576 | tf_op jit(solution)/shard_map/reshape | solution.py:329
  90.7 0.1 fusion.35
  90.8 0.0 collective-permute-done.3
  90.8 0.1 fusion.32
  90.9 1.5 %add_convert_fusion = bf16[128,2048]{1,0:T(8,128)(2,1)S(1)} fusion(f32[512,2048]{1,0:T(8,128)} %get-tuple-element.8, s32[]{:T(128)S(6)} %select_n.50, f16[136,2048]{1,0:T(8,128)(2,1)S(1)} %collective-permute-done.5, f16[136,2048]{1,0:T(8,128)(2,1)S(1)} %collective-permute-done.3, f32[2048]{0:T(1024)S(1)} %bitcast.24, f32[2048]{0:T(1024)S(1)} %bitcast.29), kind=kLoop, calls=%fused_computation | loop fusion | flops 1835008 | bytes 2637828 | tf_op jit(solution)/shard_map/convert_element_type | solution.py:329
  92.3 1.2 %reshape.21 = bf16[128,4,512]{2,1,0:T(4,128)(2,1)} reshape(bf16[128,2048]{1,0:T(8,128)(2,1)S(1)} %add_convert_fusion) | data formatting | bytes 1048576 | tf_op jit(solution)/shard_map/reshape | solution.py:329
  (27 shorter events, 0.3 us)
Async XLA Ops:
  1.8 26.9 %copy-start.2 = (bf16[16,8,4,512]{3,1,2,0:T(8,128)(2,1)}, bf16[16,8,4,512]{3,1,2,0:T(8,128)(2,1)S(1)}, u32[]{:S(2)}) copy-start(bf16[16,8,4,512]{3,1,2,0:T(8,128)(2,1)S(1)} %copy.6) | copy-start | bytes 1572868
  1.8 29.2 %collective-permute-start.6 = (bf16[128,2048]{1,0:T(8,128)(2,1)S(1)}, bf16[128,2048]{1,0:T(8,128)(2,1)S(1)}, u32[]{:S(2)}, u32[]{:S(2)}) collective-permute-start(bf16[128,2048]{1,0:T(8,128)(2,1)S(1)} %bitcast.14), channel_id=1, source_target_pairs={{8,0},{16,8},{24,16},{9,1},{17,9},{25,17},{10,2},{18,10},{26,18},{... | collective-permute-start | bytes 1572872 | tf_op jit(solution)/shard_map/ppermute | solution.py:283
  3.1 27.9 %collective-permute-start.7 = (bf16[128,2048]{1,0:T(8,128)(2,1)S(1)}, bf16[128,2048]{1,0:T(8,128)(2,1)}, u32[]{:S(2)}, u32[]{:S(2)}) collective-permute-start(bf16[128,2048]{1,0:T(8,128)(2,1)S(1)} %bitcast.15), channel_id=1, source_target_pairs={{0,8},{8,16},{16,24},{1,9},{9,17},{17,25},{2,10},{10,18},{18,26},{... | collective-permute-start | bytes 1572872 | tf_op jit(solution)/shard_map/ppermute | solution.py:283
  10.6 1.7 %copy-start.4 = (bf16[16,8,4,512]{3,1,2,0:T(8,128)(2,1)}, bf16[16,8,4,512]{3,1,2,0:T(8,128)(2,1)S(1)}, u32[]{:S(2)}) copy-start(bf16[16,8,4,512]{3,1,2,0:T(8,128)(2,1)S(1)} %copy.5) | copy-start | bytes 1572868
  10.7 1.6 %collective-permute-start = (bf16[128,1024]{1,0:T(8,128)(2,1)S(1)}, bf16[128,1024]{1,0:T(8,128)(2,1)S(1)}, u32[]{:S(2)}, u32[]{:S(2)}) collective-permute-start(bf16[128,1024]{1,0:T(8,128)(2,1)S(1)} %pad_maximum_fusion.4), channel_id=1, source_target_pairs={{0,4},{4,0},{1,5},{5,1},{2,6},{6,2},{3,7},{7,3},{8,12},{12,8},{9,1... | collective-permute-start | bytes 786440 | tf_op jit(solution)/shard_map/ppermute | solution.py:245
  10.8 27.1 %collective-permute-start.10 = (bf16[128,1024]{1,0:T(8,128)(2,1)S(1)}, bf16[128,1024]{1,0:T(8,128)(2,1)S(1)}, u32[]{:S(2)}, u32[]{:S(2)}) collective-permute-start(bf16[128,1024]{1,0:T(8,128)(2,1)S(1)} %pad_maximum_fusion.5), channel_id=1, source_target_pairs={{0,4},{4,0},{1,5},{5,1},{2,6},{6,2},{3,7},{7,3},{8,12},{12,8},{9,1... | collective-permute-start | bytes 786440 | tf_op jit(solution)/shard_map/ppermute | solution.py:245
  12.3 0.7 copy-start.8
  31.0 6.9 %copy-start.3 = (bf16[128,2048]{1,0:T(8,128)(2,1)}, bf16[128,2048]{1,0:T(8,128)(2,1)S(1)}, u32[]{:S(2)}) copy-start(bf16[128,2048]{1,0:T(8,128)(2,1)S(1)} %broadcast_select_fusion.1.refs_3_) | copy-start | bytes 1572868
  31.1 6.9 %collective-permute-start.11 = (bf16[128,1024]{1,0:T(8,128)(2,1)S(1)}, bf16[128,1024]{1,0:T(8,128)(2,1)}, u32[]{:S(2)}, u32[]{:S(2)}) collective-permute-start(bf16[128,1024]{1,0:T(8,128)(2,1)S(1)} %pad_maximum_fusion.6), channel_id=1, source_target_pairs={{0,4},{4,0},{1,5},{5,1},{2,6},{6,2},{3,7},{7,3},{8,12},{12,8},{9,1... | collective-permute-start | bytes 786440 | tf_op jit(solution)/shard_map/ppermute | solution.py:245
  31.4 16.6 %collective-permute-start.1 = (f16[136,2048]{1,0:T(8,128)(2,1)S(1)}, f16[136,2048]{1,0:T(8,128)(2,1)S(1)}, u32[]{:S(2)}, u32[]{:S(2)}) collective-permute-start(f16[136,2048]{1,0:T(8,128)(2,1)S(1)} %pad_maximum_fusion), channel_id=1, source_target_pairs={{0,8},{24,16},{1,9},{25,17},{2,10},{26,18},{3,11},{27,19},{4,12},{... | collective-permute-start | bytes 1671176 | tf_op jit(solution)/shard_map/ppermute | solution.py:283
  35.7 12.5 %copy-start = (f32[512,2048]{1,0:T(8,128)S(1)}, f32[512,2048]{1,0:T(8,128)}, u32[]{:S(2)}) copy-start(f32[512,2048]{1,0:T(8,128)} %get-tuple-element.8) | copy-start | bytes 12582916
  35.7 18.8 %collective-permute-start.8 = (bf16[128,2048]{1,0:T(8,128)(2,1)}, bf16[128,2048]{1,0:T(8,128)(2,1)S(1)}, u32[]{:S(2)}, u32[]{:S(2)}) collective-permute-start(bf16[128,2048]{1,0:T(8,128)(2,1)} %collective-permute-done.7), channel_id=1, source_target_pairs={{8,16},{16,24},{9,17},{17,25},{10,18},{18,26},{11,19},{19,27},{12,... | collective-permute-start | bytes 1572872 | tf_op jit(solution)/shard_map/ppermute | solution.py:283
  36.5 17.9 %collective-permute-start.9 = (bf16[128,2048]{1,0:T(8,128)(2,1)S(1)}, bf16[128,2048]{1,0:T(8,128)(2,1)S(1)}, u32[]{:S(2)}, u32[]{:S(2)}) collective-permute-start(bf16[128,2048]{1,0:T(8,128)(2,1)S(1)} %collective-permute-done.6), channel_id=1, source_target_pairs={{16,8},{8,0},{17,9},{9,1},{18,10},{10,2},{19,11},{11,3},{20,12},{1... | collective-permute-start | bytes 1572872 | tf_op jit(solution)/shard_map/ppermute | solution.py:283
  38.0 0.7 copy-start.6
  48.5 7.5 %collective-permute-start.4 = (f16[136,2048]{1,0:T(8,128)(2,1)S(1)}, f16[136,2048]{1,0:T(8,128)(2,1)S(1)}, u32[]{:S(2)}, u32[]{:S(2)}) collective-permute-start(f16[136,2048]{1,0:T(8,128)(2,1)S(1)} %pad_maximum_fusion.1), channel_id=1, source_target_pairs={{24,16},{16,8},{25,17},{17,9},{26,18},{18,10},{27,19},{19,11},{28,... | collective-permute-start | bytes 1671176 | tf_op jit(solution)/shard_map/ppermute | solution.py:283
  49.2 17.3 %collective-permute-start.2 = (f16[136,2048]{1,0:T(8,128)(2,1)S(1)}, f16[136,2048]{1,0:T(8,128)(2,1)S(1)}, u32[]{:S(2)}, u32[]{:S(2)}) collective-permute-start(f16[136,2048]{1,0:T(8,128)(2,1)S(1)} %pad_maximum_fusion.1), channel_id=1, source_target_pairs={{0,8},{8,16},{1,9},{9,17},{2,10},{10,18},{3,11},{11,19},{4,12},{12... | collective-permute-start | bytes 1671176 | tf_op jit(solution)/shard_map/ppermute | solution.py:283
  54.6 16.8 %copy-start.1 = (bf16[128,2048]{1,0:T(8,128)(2,1)}, bf16[128,2048]{1,0:T(8,128)(2,1)S(1)}, u32[]{:S(2)}) copy-start(bf16[128,2048]{1,0:T(8,128)(2,1)S(1)} %get-tuple-element.14.refs_2_) | copy-start | bytes 1572868
  54.6 23.1 %collective-permute-start.12 = (bf16[128,1024]{1,0:T(8,128)(2,1)S(1)}, bf16[128,1024]{1,0:T(8,128)(2,1)S(1)}, u32[]{:S(2)}, u32[]{:S(2)}) collective-permute-start(bf16[128,1024]{1,0:T(8,128)(2,1)S(1)} %pad_maximum_fusion.7), channel_id=1, source_target_pairs={{0,4},{4,0},{1,5},{5,1},{2,6},{6,2},{3,7},{7,3},{8,12},{12,8},{9,1... | collective-permute-start | bytes 786440 | tf_op jit(solution)/shard_map/ppermute | solution.py:245
  54.7 16.5 %collective-permute-start.13 = (bf16[128,2048]{1,0:T(8,128)(2,1)S(1)}, bf16[128,2048]{1,0:T(8,128)(2,1)S(1)}, u32[]{:S(2)}, u32[]{:S(2)}) collective-permute-start(bf16[128,2048]{1,0:T(8,128)(2,1)S(1)} %get-tuple-element.15), channel_id=1, source_target_pairs={{16,24},{8,0},{17,25},{9,1},{18,26},{10,2},{19,27},{11,3},{20,28},... | collective-permute-start | bytes 1572872 | tf_op jit(solution)/shard_map/ppermute | solution.py:283
  71.3 6.5 %copy-start.5 = (bf16[128,2048]{1,0:T(8,128)(2,1)}, bf16[128,2048]{1,0:T(8,128)(2,1)S(1)}, u32[]{:S(2)}) copy-start(bf16[128,2048]{1,0:T(8,128)(2,1)S(1)} %broadcast_select_fusion.2.refs_3_) | copy-start | bytes 1572868
  71.3 6.4 %collective-permute-start.14 = (bf16[128,1024]{1,0:T(8,128)(2,1)S(1)}, bf16[128,1024]{1,0:T(8,128)(2,1)S(1)}, u32[]{:S(2)}, u32[]{:S(2)}) collective-permute-start(bf16[128,1024]{1,0:T(8,128)(2,1)S(1)} %pad_maximum_fusion.8), channel_id=1, source_target_pairs={{0,4},{4,0},{1,5},{5,1},{2,6},{6,2},{3,7},{7,3},{8,12},{12,8},{9,1... | collective-permute-start | bytes 786440 | tf_op jit(solution)/shard_map/ppermute | solution.py:245
  71.6 19.1 %collective-permute-start.5 = (f16[136,2048]{1,0:T(8,128)(2,1)S(1)}, f16[136,2048]{1,0:T(8,128)(2,1)S(1)}, u32[]{:S(2)}, u32[]{:S(2)}) collective-permute-start(f16[136,2048]{1,0:T(8,128)(2,1)S(1)} %pad_maximum_fusion.3), channel_id=1, source_target_pairs={{24,16},{16,8},{8,0},{25,17},{17,9},{9,1},{26,18},{18,10},{10,2},{... | collective-permute-start | bytes 1671176 | tf_op jit(solution)/shard_map/ppermute | solution.py:283
  73.0 17.8 %collective-permute-start.3 = (f16[136,2048]{1,0:T(8,128)(2,1)S(1)}, f16[136,2048]{1,0:T(8,128)(2,1)S(1)}, u32[]{:S(2)}, u32[]{:S(2)}) collective-permute-start(f16[136,2048]{1,0:T(8,128)(2,1)S(1)} %pad_maximum_fusion.2), channel_id=1, source_target_pairs={{0,8},{8,16},{16,24},{1,9},{9,17},{17,25},{2,10},{10,18},{18,26},{... | collective-permute-start | bytes 1671176 | tf_op jit(solution)/shard_map/ppermute | solution.py:283
  77.8 0.7 copy-start.7
  78.5 0.7 copy-start.9

commit v2 on v1

--- a/solution.py
+++ b/solution.py
@@ -10,7 +10,8 @@
 
 NZ = 64
 OFFSETS = (-1, 0, 1)
-VMEM_LIMIT = 56 * 2**20
+FORWARD_VMEM = 28 * 2**20
+BACKWARD_VMEM = 28 * 2**20
 
 
 def shift_z(block, offset):
@@ -75,8 +76,7 @@
         high = jnp.maximum(power, -14.0)
         row = lax.broadcasted_iota(jnp.int32, top_ref.shape, 0) - 2 * position_ref[0]
         mark = jnp.where(row == 0, jnp.exp2(high), jnp.where(row == 1, jnp.exp2(power - high), 0.0))
-        for lane in range(0, marks_ref.shape[1], mark.shape[1]):
-            marks_ref[:, lane : lane + mark.shape[1]] = mark
+        marks_ref[...] = mark
 
 
 def forward(position, x, halo, w, slab):
@@ -92,7 +92,7 @@
             in_specs=[whole(halo), whole(x), whole(w)],
             out_specs=[
                 pl.BlockSpec((full, size), lambda n, s: (0, n)),
-                pl.BlockSpec((8, cells), lambda n, s: (0, 0)),
+                pl.BlockSpec((8, 128), lambda n, s: (0, 0)),
             ],
             scratch_shapes=[
                 pltpu.VMEM((9 * chans, (slab + 2) * size), jnp.bfloat16),
@@ -102,9 +102,9 @@
         ),
         out_shape=[
             jax.ShapeDtypeStruct((full, cells), jnp.float32),
-            jax.ShapeDtypeStruct((8, cells), jnp.float32),
+            jax.ShapeDtypeStruct((8, 128), jnp.float32),
         ],
-        compiler_params=pltpu.CompilerParams(vmem_limit_bytes=VMEM_LIMIT),
+        compiler_params=pltpu.CompilerParams(vmem_limit_bytes=FORWARD_VMEM),
         cost_estimate=pl.CostEstimate(
             flops=2 * 27 * chans * full * cells,
             bytes_accessed=w.size * 2 + full * cells * 4,
@@ -173,7 +173,7 @@
             scratch_shapes=[pltpu.VMEM((9 * chans_in, 3 * number * chans), jnp.bfloat16),
                             pltpu.VMEM((3 * number * chans, cells), jnp.bfloat16)]),
         out_shape=jax.ShapeDtypeStruct((chans_in, cells), out_dtype),
-        compiler_params=pltpu.CompilerParams(vmem_limit_bytes=VMEM_LIMIT),
+        compiler_params=pltpu.CompilerParams(vmem_limit_bytes=BACKWARD_VMEM),
         cost_estimate=pl.CostEstimate(flops=2*27*chans*chans_in*cells*number, bytes_accessed=w.size*2+chans_in*cells*4, transcendentals=0),
         name="backward",
     )(position, *args)
@@ -250,6 +250,18 @@
 
 LINE = 4
 TOP = 32768.0
+ROWS, LANES = 8, 128
+
+
+def tiles(block):
+    rows, columns = block.shape
+    split = block.reshape(rows // ROWS, ROWS, columns // LANES, LANES)
+    return split.transpose(0, 2, 1, 3).reshape(-1, LANES)
+
+
+def untiled(block, rows):
+    split = block.reshape(rows // ROWS, -1, ROWS, LANES)
+    return split.transpose(0, 2, 1, 3).reshape(rows, -1)
 
 
 def scale_of(marks):
@@ -263,70 +275,82 @@
 
 
 def unpack(parcel):
-    rows = parcel.shape[0] - 2 * LINE
-    return parcel[:rows].astype(jnp.float32) * (scale_of(parcel[rows:]) * (1.0 / TOP)), parcel[rows:]
-
-
-def pack_sum(total, marks, parcel):
-    other, other_marks = unpack(parcel)
-    return pack(total + other, marks + other_marks)
+    return parcel[:-ROWS].astype(jnp.float32) * (scale_of(parcel[-ROWS:]) * (1.0 / TOP))
 
 
 def line_of_four(inputs, weights, out_grad):
     chans, slab_len, size = inputs.shape
     cells = slab_len * size
+    slabs = lax.axis_size("slab")
     place = lax.axis_index("chan")
     position = place.reshape(1)
-    middle = (place == 1) | (place == 2)
-
-    def move(block, pairs):
-        return lax.ppermute(block, "chan", pairs)
+    inner = (place == 1) | (place == 2)
+
+    def swap_ends(block):
+        return lax.ppermute(block, "chan", [(0, 1), (1, 0), (2, 3), (3, 2)])
+
+    def swap_middle(block):
+        pairs = []
+        for slab in range(slabs):
+            other = (slab + 1) % slabs
+            pairs += [(slabs + slab, 2 * slabs + slab), (2 * slabs + slab, slabs + slab)]
+            pairs += [(end * slabs + slab, end * slabs + other) for end in (0, 3)]
+        return lax.ppermute(block, ("chan", "slab"), pairs)
+
+    def block(index):
+        return lax.dynamic_index_in_dim(partial, index, axis=0, keepdims=False)
+
+    def partial_or_cotangent(index, cotangent):
+        cotangent = tiles(cotangent).astype(jnp.float32)
+        bound = jnp.maximum(jnp.max(jnp.abs(cotangent), axis=0, keepdims=True) * 1.01, 2.0**-14)
+        row = lax.broadcasted_iota(jnp.int32, marks.shape, 0)
+        bounds = jnp.where(row == 0, bound, jnp.where(row == 1, 1.0, 0.0)).astype(jnp.float16)
+        return pack(jnp.where(inner, cotangent, block(index)), jnp.where(inner, bounds, marks))
+
+    def sum_with(index, parcel, counts=True):
+        others = jnp.where(counts, parcel[-ROWS:], jnp.zeros_like(marks))
+        theirs = parcel[:-ROWS].astype(jnp.float32) * (scale_of(others) * (1.0 / TOP))
+        return pack(block(index) + theirs, marks + others)
+
+    def cotangent_of(parcel):
+        return untiled(unpack(parcel).astype(jnp.bfloat16), chans)
 
     grad = out_grad.reshape(chans, cells)
     field = inputs.reshape(chans, cells)
-    from_below = move(grad, [(0, 1), (1, 2), (2, 3)])
-    from_above = move(grad, [(1, 0), (2, 1), (3, 2)])
+    ends_1 = swap_ends(grad)
+    middle_1 = swap_middle(grad)
     field_edges = edge_planes(field, size)
     grad_edges = edge_planes(grad, size)
 
     partial, marks = forward(position, field, field_edges, weights, slab_len)
+    partial = tiles(partial).reshape(LINE, -1, LANES)
     marks = marks.astype(jnp.float16)
-    block = lambda index: lax.dynamic_slice_in_dim(partial, index * chans, chans, axis=0)
-
-    sum_1 = move(pack(block(jnp.where(place < 2, 3, 0)), marks), [(0, 1), (3, 2)])
-    below_2 = move(from_below, [(1, 2), (2, 3)])
-    above_2 = move(from_above, [(2, 1), (1, 0)])
-    second = jnp.where(place == 0, from_above, from_below)
-    second_edges = edge_planes(second, size)
+
+    middle_2 = swap_middle(ends_1)
+    ends_2 = swap_ends(partial_or_cotangent(jnp.where(place < 2, 3, 0), middle_1))
+    second_edges = edge_planes(ends_1, size)
     grad_half = backward(
-        position, (own_place, second_place), (grad, second), (grad_edges, second_edges),
+        position, (own_place, second_place), (grad, ends_1), (grad_edges, second_edges),
         weights, None, slab_len, jnp.float32,
     )
 
-    parcel = pack_sum(block((place + 2) % 4), marks, sum_1)
-    sum_below = move(parcel, [(0, 1), (1, 2)])
-    sum_above = move(parcel, [(3, 2), (2, 1)])
-    from_above, below_2, above_2, grad_half = lax.optimization_barrier(
-        (from_above, below_2, above_2, grad_half)
-    )
-    relayed = jnp.where(place >= 2, below_2, above_2)
-    far = move(relayed, [(2, 3), (1, 0)])
-    third = jnp.where(middle, from_above, relayed)
-    fourth = jnp.where(middle, relayed, far)
+    ends_3 = swap_ends(partial_or_cotangent(jnp.where(place < 2, 2, 1), middle_2))
+    middle_3 = swap_middle(sum_with(jnp.where(place < 2, 3, 0), ends_2))
+    third = jnp.where(inner, middle_1, cotangent_of(ends_2))
     third_edges = edge_planes(third, size)
+
+    ends_4 = swap_ends(sum_with(place ^ 1, middle_3, inner))
+    middle_4 = swap_middle(sum_with(jnp.where(place < 2, 2, 1), ends_3))
+    fourth = jnp.where(inner, middle_2, cotangent_of(ends_3))
     fourth_edges = edge_planes(fourth, size)
-
-    upward = pack_sum(block(jnp.minimum(place + 1, 3)), marks, sum_below)
-    downward = pack_sum(block(jnp.maximum(place - 1, 0)), marks, sum_above)
-    last_below = move(upward, [(0, 1), (1, 2), (2, 3)])
-    last_above = move(downward, [(3, 2), (2, 1), (1, 0)])
     input_grad = backward(
         position, (third_place, fourth_place), (third, fourth), (third_edges, fourth_edges),
         weights, grad_half, slab_len, jnp.bfloat16,
     )
-    conv_out = block(place) + unpack(last_below)[0] + unpack(last_above)[0]
+    conv_out = block(place) + unpack(ends_4) + jnp.where(inner, unpack(middle_4), 0.0)
+    conv_out = untiled(conv_out.astype(jnp.bfloat16), chans)
     shape = (chans, slab_len, size)
-    return conv_out.astype(jnp.bfloat16).reshape(shape), input_grad.reshape(shape)
+    return conv_out.reshape(shape), input_grad.reshape(shape)
 
 
 def own_place(place):
@@ -334,11 +358,11 @@
 
 
 def second_place(place):
-    return jnp.where(place == 0, 1, place - 1)
+    return place ^ 1
 
 
 def third_place(place):
-    return jnp.where(place == 3, 1, jnp.where(place == 2, 3, 2))
+    return jnp.where(place < 2, 2, 1)
 
 
 def fourth_place(place):

time: 94.2 us -> 73 us (0.77)
  starting transfers between devices: 28.4 us -> 9.84 us
  waiting for transfers between devices: 15.5 us -> 26.3 us
  Pallas kernels: 34.2 us -> 24.8 us
  local copies, waits for them, and re-layouts: 8.6 us -> 6.67 us
  other arithmetic: 5.7 us -> 4.17 us
    ppermute x10 -> x8, starting transfers between devices: 27.4 us -> 8.87 us  [the longest x4 7.51 us: swap_ends(): return lax.ppermute(block, 'chan', [(0, 1), (1, 0), (2, 3), (3, 2)])]
    ppermute x10 -> x8, waiting for transfers between devices: 14.6 us -> 24.8 us  [the longest x4 24.8 us: swap_ends(): return lax.ppermute(block, 'chan', [(0, 1), (1, 0), (2, 3), (3, 2)])]
    pallas_call x2, Pallas kernels: 18.5 us -> 12.1 us  [backward(): pl.pallas_call(functools.partial(backward_kernel, slab, sources, first),...]
    pallas_call x1, Pallas kernels: 15.7 us -> 12.7 us  [forward(): pl.pallas_call(functools.partial(forward_kernel, slab), grid_spec=pltpu.P...]
    reshape x2 -> x1, local copies, waits for them, and re-layouts: 3.39 us -> 1.17 us  [line_of_four(): return (conv_out.reshape(shape), input_grad.reshape(shape))]
    another operation x0 -> x1, local copies, waits for them, and re-layouts: none -> 1 us  [line_of_four(): return (conv_out.reshape(shape), input_grad.reshape(shape))]
    unnamed x22 -> x6, local copies, waits for them, and re-layouts: 5.11 us -> 4.29 us
  transfers between devices with their start and end apart: 15 -> 13, of which waited for: 4 -> 5; matrix products, arithmetic and copies ran while one was open for 8% -> 6% of each run, Pallas kernels for 37% -> 34%
where the time goes in v2:
time: 73 us; the launch traced here: 72.7 us
  waiting for transfers between devices  26.3 us (36%)
  Pallas kernels  24.8 us (34%)
  starting transfers between devices  9.84 us (13%)
  local copies, waits for them, and re-layouts  6.67 us (9%)
  other arithmetic  4.17 us (6%)
  between operations  0.97 us (1%)
    ppermute x4, waiting for transfers between devices, swap_ends(): return lax.ppermute(block, 'chan', [(0, 1), (1, 0), (2, 3), (3, 2)])  24.8 us
    pallas_call x1, Pallas kernels, forward(): pl.pallas_call(functools.partial(forward_kernel, slab), grid_spec=pltpu.P...  12.7 us
    pallas_call x2, Pallas kernels, backward(): pl.pallas_call(functools.partial(backward_kernel, slab, sources, first),...  12.1 us
    ppermute x4, starting transfers between devices, swap_ends(): return lax.ppermute(block, 'chan', [(0, 1), (1, 0), (2, 3), (3, 2)])  7.51 us
    unnamed x6, local copies, waits for them, and re-layouts  4.29 us
    convert_element_type x1, other arithmetic, line_of_four(): conv_out = untiled(conv_out.astype(jnp.bfloat16), chans)  1.53 us
    ppermute x5, waiting for transfers between devices, edge_planes(): return lax.ppermute(jnp.concatenate([last, first], axis=1), 'slab', upward)  1.49 us
  transfers between devices with their start and end apart: 13, of which 5 were waited for; matrix products, arithmetic and copies ran while one was open for 6% of the time, Pallas kernels for 34%

profile of v2, /device:TPU:0, one launch (start us, length us, event | category | flops | bytes accessed | tf_op | source)
XLA Modules:
  0.0 72.7 jit_solution(18031466864155500652)
XLA Ops:
  0.6 1.1 %copy.8 = bf16[16,8,4,512]{3,1,2,0:T(8,128)(2,1)S(1)} copy(bf16[16,8,4,512]{3,2,1,0:T(4,128)(2,1)} %bitcast.108) | data formatting | bytes 1048576
  1.8 0.6 collective-permute-start.1
  2.3 4.1 %collective-permute-start.5 = (bf16[128,2048]{1,0:T(8,128)(2,1)S(1)}, bf16[128,2048]{1,0:T(8,128)(2,1)S(1)}, u32[]{:S(2)}, u32[]{:S(2)}) collective-permute-start(bf16[128,2048]{1,0:T(8,128)(2,1)S(1)} %bitcast.98), channel_id=1, source_target_pairs={{0,8},{8,0},{16,24},{24,16},{1,9},{9,1},{17,25},{25,17},{2,10},{10... | collective-permute-start | bytes 1572872 | tf_op jit(solution)/shard_map/ppermute | solution.py:290
  6.5 1.1 %copy.7 = bf16[16,8,4,512]{3,1,2,0:T(8,128)(2,1)S(1)} copy(bf16[16,8,4,512]{3,2,1,0:T(4,128)(2,1)} %bitcast.109) | data formatting | bytes 1048576
  7.7 0.1 collective-permute-start
  7.8 0.6 collective-permute-start.11
  8.4 0.9 %collective-permute-done.halo_ref = bf16[128,1024]{1,0:T(8,128)(2,1)S(1)} collective-permute-done((bf16[128,1024]{1,0:T(8,128)(2,1)S(1)}, bf16[128,1024]{1,0:T(8,128)(2,1)S(1)}, u32[]{:S(2)}, u32[]{:S(2)}) %collective-permute-start) | collective-permute-done | bytes 262176 | tf_op jit(solution)/shard_map/ppermute | solution.py:245
  9.3 0.0 copy-start.1
  9.3 2.0 %copy-done.1 = bf16[27,128,512]{2,1,0:T(8,128)(2,1)S(1)} copy-done((bf16[27,128,512]{2,1,0:T(8,128)(2,1)S(1)}, bf16[27,128,512]{2,1,0:T(8,128)(2,1)}, u32[]{:S(2)}) %copy-start.1) | copy-done | bytes 3538968
  11.3 12.7 %forward.1 = (f32[512,2048]{1,0:T(8,128)S(1)}, f32[8,128]{1,0:T(8,128)S(1)}) custom-call(s32[1]{0:T(128)} %bitcast.position_ref, bf16[128,1024]{1,0:T(8,128)(2,1)S(1)} %collective-permute-done.halo_ref, bf16[128,2048]{1,0:T(8,128)(2,1)S(1)} %bitcast.102, bf16[27,128,512]{2,1,0:T(8,128)(2,1)S(1)} %copy-done.1), custom_call_target="tpu_custom_call" | custom-call | flops 7247757312 | bytes 7733248 | tf_op jit(solution)/shard_map/forward/pallas_call | solution.py:87
  24.0 0.0 copy-start
  24.0 0.0 collective-permute-done.1
  24.0 0.1 abs_reduce_fusion.1
  24.1 0.1 fusion.21
  24.2 0.0 collective-permute-done.5.refs_3_
  24.3 0.2 collective-permute-start.12
  24.4 0.1 convert_element_type.156
  24.5 0.2 fusion.5
  24.7 0.4 collective-permute-start.6
  25.2 0.1 pad_maximum_fusion
  25.3 1.4 %collective-permute-start.2 = (f16[2056,128]{1,0:T(8,128)(2,1)S(1)}, f16[2056,128]{1,0:T(8,128)(2,1)S(1)}, u32[]{:S(2)}, u32[]{:S(2)}) collective-permute-start(f16[2056,128]{1,0:T(8,128)(2,1)S(1)} %pad_maximum_fusion), channel_id=1, source_target_pairs={{0,8},{8,0},{16,24},{24,16},{1,9},{9,1},{17,25},{25,17},{2,10},{10... | collective-permute-start | bytes 1579016 | tf_op jit(solution)/shard_map/ppermute | solution.py:290
  26.7 0.0 collective-permute-done.11.refs_0_
  26.7 0.0 collective-permute-done.12.refs_1_
  26.7 6.0 %backward.2.refs_5_ = f32[128,2048]{1,0:T(8,128)S(1)} custom-call(s32[1]{0:T(128)} %bitcast.position_ref, bf16[128,1024]{1,0:T(8,128)(2,1)S(1)} %collective-permute-done.11.refs_0_, bf16[128,1024]{1,0:T(8,128)(2,1)S(1)} %collective-permute-done.12.refs_1_, bf16[128,2048]{1,0:T(8,128)(2,1)S(1)} %bitcast.100, ...), custom_call_target="tpu_custom_call" | custom-call | flops 3623878656 | bytes 4587520 | tf_op jit(solution)/shard_map/backward/pallas_call | solution.py:167
  32.7 0.0 collective-permute-done.6
  32.7 0.1 convert_element_type.157
  32.8 0.1 abs_reduce_fusion
  32.9 6.5 %collective-permute-done.2 = f16[2056,128]{1,0:T(8,128)(2,1)S(1)} collective-permute-done((f16[2056,128]{1,0:T(8,128)(2,1)S(1)}, f16[2056,128]{1,0:T(8,128)(2,1)S(1)}, u32[]{:S(2)}, u32[]{:S(2)}) %collective-permute-start.2) | collective-permute-done | bytes 526368 | tf_op jit(solution)/shard_map/ppermute | solution.py:290
  39.4 0.1 fusion.20
  39.5 0.4 fusion.7
  39.9 0.1 pad_maximum_fusion.1
  40.1 0.1 collective-permute-start.3
  40.1 0.1 pad_maximum_fusion.3
  40.3 1.7 %collective-permute-start.7 = (f16[2056,128]{1,0:T(8,128)(2,1)S(1)}, f16[2056,128]{1,0:T(8,128)(2,1)S(1)}, u32[]{:S(2)}, u32[]{:S(2)}) collective-permute-start(f16[2056,128]{1,0:T(8,128)(2,1)S(1)} %pad_maximum_fusion.3), channel_id=1, source_target_pairs={{0,8},{8,0},{16,24},{24,16},{1,9},{9,1},{17,25},{25,17},{2,10},{10... | collective-permute-start | bytes 1579016 | tf_op jit(solution)/shard_map/ppermute | solution.py:290
  42.0 0.1 broadcast_select_fusion.1.refs_2_
  42.1 0.1 collective-permute-start.9
  42.1 0.0 collective-permute-done.3
  42.2 12.6 %collective-permute-done.7 = f16[2056,128]{1,0:T(8,128)(2,1)S(1)} collective-permute-done((f16[2056,128]{1,0:T(8,128)(2,1)S(1)}, f16[2056,128]{1,0:T(8,128)(2,1)S(1)}, u32[]{:S(2)}, u32[]{:S(2)}) %collective-permute-start.7) | collective-permute-done | bytes 526368 | tf_op jit(solution)/shard_map/ppermute | solution.py:290
  54.8 0.0 copy-done
  54.8 0.5 fusion.9
  55.3 0.1 broadcast_select_fusion.refs_3_
  55.4 0.1 collective-permute-start.10
  55.5 0.1 pad_maximum_fusion.2
  55.6 0.4 collective-permute-start.4
  56.0 0.1 pad_maximum_fusion.4
  56.1 0.3 collective-permute-start.8
  56.4 0.0 collective-permute-done.9.refs_0_
  56.4 0.6 collective-permute-done.10.refs_1_
  57.0 6.1 %backward.3 = bf16[128,2048]{1,0:T(8,128)(2,1)S(1)} custom-call(s32[1]{0:T(128)} %bitcast.position_ref, bf16[128,1024]{1,0:T(8,128)(2,1)S(1)} %collective-permute-done.9.refs_0_, bf16[128,1024]{1,0:T(8,128)(2,1)S(1)} %collective-permute-done.10.refs_1_, bf16[128,2048]{1,0:T(8,128)(2,1)S(1)} %broadcast_select_fusion.1.refs_2_, ...), custom_call_target="tpu_custom_call" | custom-call | flops 3623878656 | bytes 4587520 | tf_op jit(solution)/shard_map/backward/pallas_call | solution.py:167
  63.1 1.2 %reshape.73 = bf16[128,4,512]{2,1,0:T(4,128)(2,1)} reshape(bf16[128,2048]{1,0:T(8,128)(2,1)S(1)} %backward.3) | data formatting | bytes 1048576 | tf_op jit(solution)/shard_map/reshape | solution.py:353
  64.3 5.8 %collective-permute-done.4 = f16[2056,128]{1,0:T(8,128)(2,1)S(1)} collective-permute-done((f16[2056,128]{1,0:T(8,128)(2,1)S(1)}, f16[2056,128]{1,0:T(8,128)(2,1)S(1)}, u32[]{:S(2)}, u32[]{:S(2)}) %collective-permute-start.4) | collective-permute-done | bytes 526368 | tf_op jit(solution)/shard_map/ppermute | solution.py:290
  70.1 0.0 collective-permute-done.8
  70.1 1.5 %fusion.11 = bf16[2048,128]{1,0:T(8,128)(2,1)S(1)} fusion(f32[4,2048,128]{2,1,0:T(8,128)} %bitcast.96, s32[]{:T(128)S(6)} %select_n.88, f16[2056,128]{1,0:T(8,128)(2,1)S(1)} %collective-permute-done.8, f16[2056,128]{1,0:T(8,128)(2,1)S(1)} %collective-permute-done.4, f32[128]{0:T(128)S(1)} %multiply_bitcast_fusion, f32[128]{0:T(128)S(1)} %multiply_bitcast_fusion.2, ...), kind=kLoop, calls=%fused_computation.17 | loop fusion | flops 2097152 | bytes 2622469 | tf_op jit(solution)/shard_map/convert_element_type | solution.py:351
  71.6 0.1 copy.6
  71.7 1.0 %reshape_reshape.7 = bf16[128,4,512]{2,1,0:T(4,128)(2,1)} reshape(bf16[16,8,16,128]{3,2,1,0:T(8,128)(2,1)S(1)} %copy.6) | data formatting | bytes 1048576 | tf_op jit(solution)/shard_map/reshape;reshape | solution.py:353
  (28 shorter events, 0.4 us)
Async XLA Ops:
  1.8 22.2 %collective-permute-start.1 = (bf16[128,2048]{1,0:T(8,128)(2,1)S(1)}, bf16[128,2048]{1,0:T(8,128)(2,1)S(1)}, u32[]{:S(2)}, u32[]{:S(2)}) collective-permute-start(bf16[128,2048]{1,0:T(8,128)(2,1)S(1)} %bitcast.97), channel_id=1, source_target_pairs={{8,16},{16,8},{0,4},{24,28},{12,20},{20,12},{4,0},{28,24},{9,17},{... | collective-permute-start | bytes 1572872 | tf_op jit(solution)/shard_map/ppermute | solution.py:298
  2.3 21.9 %collective-permute-start.5 = (bf16[128,2048]{1,0:T(8,128)(2,1)S(1)}, bf16[128,2048]{1,0:T(8,128)(2,1)S(1)}, u32[]{:S(2)}, u32[]{:S(2)}) collective-permute-start(bf16[128,2048]{1,0:T(8,128)(2,1)S(1)} %bitcast.98), channel_id=1, source_target_pairs={{0,8},{8,0},{16,24},{24,16},{1,9},{9,1},{17,25},{25,17},{2,10},{10... | collective-permute-start | bytes 1572872 | tf_op jit(solution)/shard_map/ppermute | solution.py:290
  7.7 1.6 %collective-permute-start = (bf16[128,1024]{1,0:T(8,128)(2,1)S(1)}, bf16[128,1024]{1,0:T(8,128)(2,1)S(1)}, u32[]{:S(2)}, u32[]{:S(2)}) collective-permute-start(bf16[128,1024]{1,0:T(8,128)(2,1)S(1)} %pad_maximum_fusion.5), channel_id=1, source_target_pairs={{0,4},{4,0},{1,5},{5,1},{2,6},{6,2},{3,7},{7,3},{8,12},{12,8},{9,1... | collective-permute-start | bytes 786440 | tf_op jit(solution)/shard_map/ppermute | solution.py:245
  7.8 18.9 %collective-permute-start.11 = (bf16[128,1024]{1,0:T(8,128)(2,1)S(1)}, bf16[128,1024]{1,0:T(8,128)(2,1)S(1)}, u32[]{:S(2)}, u32[]{:S(2)}) collective-permute-start(bf16[128,1024]{1,0:T(8,128)(2,1)S(1)} %pad_maximum_fusion.8), channel_id=1, source_target_pairs={{0,4},{4,0},{1,5},{5,1},{2,6},{6,2},{3,7},{7,3},{8,12},{12,8},{9,1... | collective-permute-start | bytes 786440 | tf_op jit(solution)/shard_map/ppermute | solution.py:245
  9.3 2.0 %copy-start.1 = (bf16[27,128,512]{2,1,0:T(8,128)(2,1)S(1)}, bf16[27,128,512]{2,1,0:T(8,128)(2,1)}, u32[]{:S(2)}) copy-start(bf16[27,128,512]{2,1,0:T(8,128)(2,1)} %refs_4_.3) | copy-start | bytes 10616836
  24.0 30.8 %copy-start = (f32[512,2048]{1,0:T(8,128)}, f32[512,2048]{1,0:T(8,128)S(1)}, u32[]{:S(2)}) copy-start(f32[512,2048]{1,0:T(8,128)S(1)} %get-tuple-element.4) | copy-start | bytes 12582916
  24.3 2.4 %collective-permute-start.12 = (bf16[128,1024]{1,0:T(8,128)(2,1)S(1)}, bf16[128,1024]{1,0:T(8,128)(2,1)S(1)}, u32[]{:S(2)}, u32[]{:S(2)}) collective-permute-start(bf16[128,1024]{1,0:T(8,128)(2,1)S(1)} %pad_maximum_fusion.9), channel_id=1, source_target_pairs={{0,4},{4,0},{1,5},{5,1},{2,6},{6,2},{3,7},{7,3},{8,12},{12,8},{9,1... | collective-permute-start | bytes 786440 | tf_op jit(solution)/shard_map/ppermute | solution.py:245
  24.7 8.0 %collective-permute-start.6 = (bf16[128,2048]{1,0:T(8,128)(2,1)S(1)}, bf16[128,2048]{1,0:T(8,128)(2,1)S(1)}, u32[]{:S(2)}, u32[]{:S(2)}) collective-permute-start(bf16[128,2048]{1,0:T(8,128)(2,1)S(1)} %collective-permute-done.5.refs_3_), channel_id=1, source_target_pairs={{8,16},{16,8},{0,4},{24,28},{12,20},{20,12},{4,0},{28,24},{9,17},{... | collective-permute-start | bytes 1572872 | tf_op jit(solution)/shard_map/ppermute | solution.py:298
  25.3 14.1 %collective-permute-start.2 = (f16[2056,128]{1,0:T(8,128)(2,1)S(1)}, f16[2056,128]{1,0:T(8,128)(2,1)S(1)}, u32[]{:S(2)}, u32[]{:S(2)}) collective-permute-start(f16[2056,128]{1,0:T(8,128)(2,1)S(1)} %pad_maximum_fusion), channel_id=1, source_target_pairs={{0,8},{8,0},{16,24},{24,16},{1,9},{9,1},{17,25},{25,17},{2,10},{10... | collective-permute-start | bytes 1579016 | tf_op jit(solution)/shard_map/ppermute | solution.py:290
  40.1 2.1 %collective-permute-start.3 = (f16[2056,128]{1,0:T(8,128)(2,1)S(1)}, f16[2056,128]{1,0:T(8,128)(2,1)S(1)}, u32[]{:S(2)}, u32[]{:S(2)}) collective-permute-start(f16[2056,128]{1,0:T(8,128)(2,1)S(1)} %pad_maximum_fusion.1), channel_id=1, source_target_pairs={{8,16},{16,8},{0,4},{24,28},{12,20},{20,12},{4,0},{28,24},{9,17},{... | collective-permute-start | bytes 1579016 | tf_op jit(solution)/shard_map/ppermute | solution.py:298
  40.3 14.4 %collective-permute-start.7 = (f16[2056,128]{1,0:T(8,128)(2,1)S(1)}, f16[2056,128]{1,0:T(8,128)(2,1)S(1)}, u32[]{:S(2)}, u32[]{:S(2)}) collective-permute-start(f16[2056,128]{1,0:T(8,128)(2,1)S(1)} %pad_maximum_fusion.3), channel_id=1, source_target_pairs={{0,8},{8,0},{16,24},{24,16},{1,9},{9,1},{17,25},{25,17},{2,10},{10... | collective-permute-start | bytes 1579016 | tf_op jit(solution)/shard_map/ppermute | solution.py:290
  42.1 14.3 %collective-permute-start.9 = (bf16[128,1024]{1,0:T(8,128)(2,1)S(1)}, bf16[128,1024]{1,0:T(8,128)(2,1)S(1)}, u32[]{:S(2)}, u32[]{:S(2)}) collective-permute-start(bf16[128,1024]{1,0:T(8,128)(2,1)S(1)} %pad_maximum_fusion.6), channel_id=1, source_target_pairs={{0,4},{4,0},{1,5},{5,1},{2,6},{6,2},{3,7},{7,3},{8,12},{12,8},{9,1... | collective-permute-start | bytes 786440 | tf_op jit(solution)/shard_map/ppermute | solution.py:245
  55.4 1.6 %collective-permute-start.10 = (bf16[128,1024]{1,0:T(8,128)(2,1)S(1)}, bf16[128,1024]{1,0:T(8,128)(2,1)S(1)}, u32[]{:S(2)}, u32[]{:S(2)}) collective-permute-start(bf16[128,1024]{1,0:T(8,128)(2,1)S(1)} %pad_maximum_fusion.7), channel_id=1, source_target_pairs={{0,4},{4,0},{1,5},{5,1},{2,6},{6,2},{3,7},{7,3},{8,12},{12,8},{9,1... | collective-permute-start | bytes 786440 | tf_op jit(solution)/shard_map/ppermute | solution.py:245
  55.6 14.4 %collective-permute-start.4 = (f16[2056,128]{1,0:T(8,128)(2,1)S(1)}, f16[2056,128]{1,0:T(8,128)(2,1)S(1)}, u32[]{:S(2)}, u32[]{:S(2)}) collective-permute-start(f16[2056,128]{1,0:T(8,128)(2,1)S(1)} %pad_maximum_fusion.2), channel_id=1, source_target_pairs={{0,8},{8,0},{16,24},{24,16},{1,9},{9,1},{17,25},{25,17},{2,10},{10... | collective-permute-start | bytes 1579016 | tf_op jit(solution)/shard_map/ppermute | solution.py:290
  56.1 14.0 %collective-permute-start.8 = (f16[2056,128]{1,0:T(8,128)(2,1)S(1)}, f16[2056,128]{1,0:T(8,128)(2,1)S(1)}, u32[]{:S(2)}, u32[]{:S(2)}) collective-permute-start(f16[2056,128]{1,0:T(8,128)(2,1)S(1)} %pad_maximum_fusion.4), channel_id=1, source_target_pairs={{8,16},{16,8},{0,4},{24,28},{12,20},{20,12},{4,0},{28,24},{9,17},{... | collective-permute-start | bytes 1579016 | tf_op jit(solution)/shard_map/ppermute | solution.py:298

commit v3 on v2

--- a/solution.py
+++ b/solution.py
@@ -31,14 +31,17 @@
     return pltpu.roll(block, (NZ * offset) % block.shape[1], 1)
 
 
-def forward_kernel(slab, position_ref, halo_ref, x_ref, w_ref, out_ref, marks_ref, columns, wt, top_ref):
+def forward_kernel(slab, sums, position_ref, halo_ref, x_ref, w_ref, *refs):
+    out_refs, (marks_ref, columns, wt, top_ref) = refs[: len(sums)], refs[len(sums) :]
     plane = pl.program_id(0)
-    chans, size = w_ref.shape[1], out_ref.shape[1]
+    chans, size = out_refs[0].shape
 
     @pl.when(plane == 0)
     def _():
-        for o in range(27):
-            wt[:, o * chans:(o + 1) * chans] = w_ref[o].T
+        for i, place in enumerate(sums):
+            at = pl.multiple_of(place(position_ref[0]) * chans, chans)
+            for o in range(27):
+                wt[i * chans:(i + 1) * chans, o * chans:(o + 1) * chans] = w_ref[o, :, pl.ds(at, chans)].T
         for p in range(slab + 2):
             if p == 0:
                 source = halo_ref[:, :size]
@@ -58,7 +61,8 @@
         part = jnp.dot(wt[:, ix * 9 * chans:(ix + 1) * 9 * chans], columns[:, pl.ds(at, size)],
                        preferred_element_type=jnp.float32)
         total = part if total is None else total + part
-    out_ref[...] = total
+    for i, out_ref in enumerate(out_refs):
+        out_ref[...] = total[i * chans:(i + 1) * chans]
     top = jnp.max(jnp.max(jnp.abs(total), axis=0, keepdims=True), axis=1, keepdims=True)
     top = jnp.broadcast_to(top, top_ref.shape)
 
@@ -79,39 +83,36 @@
         marks_ref[...] = mark
 
 
-def forward(position, x, halo, w, slab):
+def forward(position, sums, x, halo, w, slab):
     chans, cells = x.shape
-    size = cells // slab
-    full = w.shape[2]
+    number, size = len(sums), cells // slab
     whole = lambda a: pl.BlockSpec(a.shape, lambda n, s: (0,) * a.ndim, pipeline_mode=pl.Buffered(1))
-    return pl.pallas_call(
-        functools.partial(forward_kernel, slab),
+    each = pl.BlockSpec((chans, size), lambda n, s: (0, n))
+    outs = [jax.ShapeDtypeStruct((chans, cells), jnp.float32)] * number
+    outs.append(jax.ShapeDtypeStruct((8, 128), jnp.float32))
+    *partials, marks = pl.pallas_call(
+        functools.partial(forward_kernel, slab, sums),
         grid_spec=pltpu.PrefetchScalarGridSpec(
             num_scalar_prefetch=1,
             grid=(slab,),
             in_specs=[whole(halo), whole(x), whole(w)],
-            out_specs=[
-                pl.BlockSpec((full, size), lambda n, s: (0, n)),
-                pl.BlockSpec((8, 128), lambda n, s: (0, 0)),
-            ],
+            out_specs=[each] * number + [pl.BlockSpec((8, 128), lambda n, s: (0, 0))],
             scratch_shapes=[
                 pltpu.VMEM((9 * chans, (slab + 2) * size), jnp.bfloat16),
-                pltpu.VMEM((full, 27 * chans), jnp.bfloat16),
+                pltpu.VMEM((number * chans, 27 * chans), jnp.bfloat16),
                 pltpu.VMEM((8, 128), jnp.float32),
             ],
         ),
-        out_shape=[
-            jax.ShapeDtypeStruct((full, cells), jnp.float32),
-            jax.ShapeDtypeStruct((8, 128), jnp.float32),
-        ],
+        out_shape=outs,
         compiler_params=pltpu.CompilerParams(vmem_limit_bytes=FORWARD_VMEM),
         cost_estimate=pl.CostEstimate(
-            flops=2 * 27 * chans * full * cells,
-            bytes_accessed=w.size * 2 + full * cells * 4,
+            flops=2 * 27 * chans * chans * number * cells,
+            bytes_accessed=w.size * 2 + number * chans * cells * 4,
             transcendentals=0,
         ),
         name="forward",
     )(position, halo, x, w)
+    return partials, marks
 
 
 def backward_kernel(slab, sources, first, position_ref, *refs):
@@ -279,8 +280,8 @@
 
 
 def line_of_four(inputs, weights, out_grad):
-    chans, slab_len, size = inputs.shape
-    cells = slab_len * size
+    shape = inputs.shape
+    chans, slab_len, size = shape
     slabs = lax.axis_size("slab")
     place = lax.axis_index("chan")
     position = place.reshape(1)
@@ -297,60 +298,74 @@
             pairs += [(end * slabs + slab, end * slabs + other) for end in (0, 3)]
         return lax.ppermute(block, ("chan", "slab"), pairs)
 
-    def block(index):
-        return lax.dynamic_index_in_dim(partial, index, axis=0, keepdims=False)
-
-    def partial_or_cotangent(index, cotangent):
+    def partial_or_cotangent(partial, marks, cotangent):
         cotangent = tiles(cotangent).astype(jnp.float32)
         bound = jnp.maximum(jnp.max(jnp.abs(cotangent), axis=0, keepdims=True) * 1.01, 2.0**-14)
         row = lax.broadcasted_iota(jnp.int32, marks.shape, 0)
         bounds = jnp.where(row == 0, bound, jnp.where(row == 1, 1.0, 0.0)).astype(jnp.float16)
-        return pack(jnp.where(inner, cotangent, block(index)), jnp.where(inner, bounds, marks))
-
-    def sum_with(index, parcel, counts=True):
+        return pack(jnp.where(inner, cotangent, partial), jnp.where(inner, bounds, marks))
+
+    def sum_with(partial, marks, parcel, counts=True):
         others = jnp.where(counts, parcel[-ROWS:], jnp.zeros_like(marks))
         theirs = parcel[:-ROWS].astype(jnp.float32) * (scale_of(others) * (1.0 / TOP))
-        return pack(block(index) + theirs, marks + others)
+        return pack(partial + theirs, marks + others)
 
     def cotangent_of(parcel):
         return untiled(unpack(parcel).astype(jnp.bfloat16), chans)
 
-    grad = out_grad.reshape(chans, cells)
-    field = inputs.reshape(chans, cells)
+    grad = out_grad.reshape(chans, slab_len * size)
+    field = inputs.reshape(chans, slab_len * size)
     ends_1 = swap_ends(grad)
     middle_1 = swap_middle(grad)
     field_edges = edge_planes(field, size)
     grad_edges = edge_planes(grad, size)
-
-    partial, marks = forward(position, field, field_edges, weights, slab_len)
-    partial = tiles(partial).reshape(LINE, -1, LANES)
+    (first,), first_marks = forward(position, (first_sum,), field, field_edges, weights, slab_len)
+    first = tiles(first)
+    first_marks = first_marks.astype(jnp.float16)
+
+    middle_2 = swap_middle(ends_1)
+    parcel = partial_or_cotangent(first, first_marks, middle_1)
+    parcel, position_2 = lax.optimization_barrier((parcel, position))
+    ends_2 = swap_ends(parcel)
+    second_edges = edge_planes(ends_1, size)
+    partials, marks = forward(
+        position_2, (second_sum, third_sum, own_place), field, field_edges, weights, slab_len
+    )
+    second, third, own = (tiles(partial) for partial in partials)
     marks = marks.astype(jnp.float16)
 
-    middle_2 = swap_middle(ends_1)
-    ends_2 = swap_ends(partial_or_cotangent(jnp.where(place < 2, 3, 0), middle_1))
-    second_edges = edge_planes(ends_1, size)
+    ends_3 = swap_ends(partial_or_cotangent(second, marks, middle_2))
+    middle_3 = swap_middle(sum_with(first, first_marks, ends_2))
     grad_half = backward(
         position, (own_place, second_place), (grad, ends_1), (grad_edges, second_edges),
         weights, None, slab_len, jnp.float32,
     )
-
-    ends_3 = swap_ends(partial_or_cotangent(jnp.where(place < 2, 2, 1), middle_2))
-    middle_3 = swap_middle(sum_with(jnp.where(place < 2, 3, 0), ends_2))
-    third = jnp.where(inner, middle_1, cotangent_of(ends_2))
-    third_edges = edge_planes(third, size)
-
-    ends_4 = swap_ends(sum_with(place ^ 1, middle_3, inner))
-    middle_4 = swap_middle(sum_with(jnp.where(place < 2, 2, 1), ends_3))
-    fourth = jnp.where(inner, middle_2, cotangent_of(ends_3))
-    fourth_edges = edge_planes(fourth, size)
+    grad_2 = jnp.where(inner, middle_1, cotangent_of(ends_2))
+    edges_2 = edge_planes(grad_2, size)
+
+    ends_4 = swap_ends(sum_with(third, marks, middle_3, inner))
+    middle_4 = swap_middle(sum_with(second, marks, ends_3))
+    grad_3 = jnp.where(inner, middle_2, cotangent_of(ends_3))
+    edges_3 = edge_planes(grad_3, size)
     input_grad = backward(
-        position, (third_place, fourth_place), (third, fourth), (third_edges, fourth_edges),
+        position, (third_place, fourth_place), (grad_2, grad_3), (edges_2, edges_3),
         weights, grad_half, slab_len, jnp.bfloat16,
     )
-    conv_out = block(place) + unpack(ends_4) + jnp.where(inner, unpack(middle_4), 0.0)
+    conv_out = own + unpack(ends_4) + jnp.where(inner, unpack(middle_4), 0.0)
     conv_out = untiled(conv_out.astype(jnp.bfloat16), chans)
-    shape = (chans, slab_len, size)
     return conv_out.reshape(shape), input_grad.reshape(shape)
+
+
+def first_sum(place):
+    return jnp.where(place < 2, 3, 0)
+
+
+def second_sum(place):
+    return jnp.where(place < 2, 2, 1)
+
+
+def third_sum(place):
+    return place ^ 1
 
 
 def own_place(place):

time: 73 us -> 73.2 us (level)
  waiting for transfers between devices: 26.3 us -> 17.7 us
  starting transfers between devices: 9.84 us -> 13.7 us
  Pallas kernels: 24.8 us -> 28.3 us
  other arithmetic: 4.17 us -> 5.55 us
    ppermute x4, waiting for transfers between devices: 24.8 us -> 16.7 us  [swap_ends(): return lax.ppermute(block, 'chan', [(0, 1), (1, 0), (2, 3), (3, 2)])]
    ppermute x4, starting transfers between devices: 7.51 us -> 11.7 us  [swap_ends(): return lax.ppermute(block, 'chan', [(0, 1), (1, 0), (2, 3), (3, 2)])]
    pallas_call x1 -> x2, Pallas kernels: 12.7 us -> 16.1 us  [forward(): pl.pallas_call(functools.partial(forward_kernel, slab, sums), grid_spec=p...]
    convert_element_type x5 -> x6, other arithmetic: 0.17 us -> 1.51 us  [scale_of(): marks = marks.astype(jnp.float32)]
    unnamed x6 -> x10, local copies, waits for them, and re-layouts: 4.29 us -> 4.3 us
  transfers between devices with their start and end apart: 13 -> 13, of which waited for: 5 -> 4; matrix products, arithmetic and copies ran while one was open for 6% -> 8% of each run, Pallas kernels for 34% -> 39%
where the time goes in v3:
time: 73.2 us; the launch traced here: 72.9 us
  Pallas kernels  28.3 us (39%)
  waiting for transfers between devices  17.7 us (24%)
  starting transfers between devices  13.7 us (19%)
  local copies, waits for them, and re-layouts  6.68 us (9%)
  other arithmetic  5.55 us (8%)
  between operations  1.02 us (1%)
    ppermute x4, waiting for transfers between devices, swap_ends(): return lax.ppermute(block, 'chan', [(0, 1), (1, 0), (2, 3), (3, 2)])  16.7 us
    pallas_call x2, Pallas kernels, forward(): pl.pallas_call(functools.partial(forward_kernel, slab, sums), grid_spec=p...  16.1 us
    pallas_call x2, Pallas kernels, backward(): pl.pallas_call(functools.partial(backward_kernel, slab, sources, first),...  12.1 us
    ppermute x4, starting transfers between devices, swap_ends(): return lax.ppermute(block, 'chan', [(0, 1), (1, 0), (2, 3), (3, 2)])  11.7 us
    unnamed x10, local copies, waits for them, and re-layouts  4.3 us
    convert_element_type x6, other arithmetic, scale_of(): marks = marks.astype(jnp.float32)  1.51 us
    convert_element_type x1, other arithmetic, line_of_four(): conv_out = untiled(conv_out.astype(jnp.bfloat16), chans)  1.48 us
  transfers between devices with their start and end apart: 13, of which 4 were waited for; matrix products, arithmetic and copies ran while one was open for 8% of the time, Pallas kernels for 39%

profile of v3, /device:TPU:0, one launch (start us, length us, event | category | flops | bytes accessed | tf_op | source)
XLA Modules:
  0.0 72.9 jit_solution(17116260002675292137)
XLA Ops:
  0.6 1.1 %copy.7 = bf16[16,8,4,512]{3,1,2,0:T(8,128)(2,1)S(1)} copy(bf16[16,8,4,512]{3,2,1,0:T(4,128)(2,1)} %bitcast.92) | data formatting | bytes 1048576
  1.8 3.1 %collective-permute-start.5 = (bf16[128,2048]{1,0:T(8,128)(2,1)S(1)}, bf16[128,2048]{1,0:T(8,128)(2,1)S(1)}, u32[]{:S(2)}, u32[]{:S(2)}) collective-permute-start(bf16[128,2048]{1,0:T(8,128)(2,1)S(1)} %bitcast.78), channel_id=1, source_target_pairs={{0,8},{8,0},{16,24},{24,16},{1,9},{9,1},{17,25},{25,17},{2,10},{10... | collective-permute-start | bytes 1572872 | tf_op jit(solution)/shard_map/ppermute | solution.py:291
  4.9 0.0 collective-permute-start
  4.9 1.1 %copy.8 = bf16[16,8,4,512]{3,1,2,0:T(8,128)(2,1)S(1)} copy(bf16[16,8,4,512]{3,2,1,0:T(4,128)(2,1)} %bitcast.93) | data formatting | bytes 1048576
  6.1 0.6 collective-permute-start.1
  6.7 0.1 collective-permute-start.11
  6.8 1.0 %collective-permute-done.1.halo_ref = bf16[128,1024]{1,0:T(8,128)(2,1)S(1)} collective-permute-done((bf16[128,1024]{1,0:T(8,128)(2,1)S(1)}, bf16[128,1024]{1,0:T(8,128)(2,1)S(1)}, u32[]{:S(2)}, u32[]{:S(2)}) %collective-permute-start.1) | collective-permute-done | bytes 262176 | tf_op jit(solution)/shard_map/ppermute | solution.py:246
  7.8 0.0 copy-start
  7.8 2.0 %copy-done = bf16[27,128,512]{2,1,0:T(8,128)(2,1)S(1)} copy-done((bf16[27,128,512]{2,1,0:T(8,128)(2,1)S(1)}, bf16[27,128,512]{2,1,0:T(8,128)(2,1)}, u32[]{:S(2)}) %copy-start) | copy-done | bytes 3538968
  9.8 5.7 %forward.2 = (f32[128,2048]{1,0:T(8,128)S(1)}, f32[8,128]{1,0:T(8,128)S(1)}) custom-call(s32[1]{0:T(128)} %bitcast.3.position_ref, bf16[128,1024]{1,0:T(8,128)(2,1)S(1)} %collective-permute-done.1.halo_ref, bf16[128,2048]{1,0:T(8,128)(2,1)S(1)} %bitcast.83, bf16[27,128,512]{2,1,0:T(8,128)(2,1)S(1)} %copy-done), custom_call_target="tpu_custom_call" | custom-call | flops 1811939328 | bytes 4587520 | tf_op jit(solution)/shard_map/forward/pallas_call | solution.py:93
  15.6 1.2 %collective-permute-done.5.refs_3_ = bf16[128,2048]{1,0:T(8,128)(2,1)S(1)} collective-permute-done((bf16[128,2048]{1,0:T(8,128)(2,1)S(1)}, bf16[128,2048]{1,0:T(8,128)(2,1)S(1)}, u32[]{:S(2)}, u32[]{:S(2)}) %collective-permute-start.5) | collective-permute-done | bytes 524320 | tf_op jit(solution)/shard_map/ppermute | solution.py:291
  16.9 0.1 collective-permute-start.12
  16.9 0.0 collective-permute-done
  17.0 0.0 copy-start.2
  17.0 0.1 abs_reduce_fusion.1
  17.1 0.1 fusion.12
  17.2 0.1 convert_element_type.160
  17.3 0.2 multiply_convert_fusion.4
  17.4 0.1 pad_maximum_fusion
  17.6 0.0 copy-start.1
  17.6 2.8 %collective-permute-start.2 = (f16[2056,128]{1,0:T(8,128)(2,1)S(1)}, f16[2056,128]{1,0:T(8,128)(2,1)S(1)}, u32[]{:S(2)}, u32[]{:S(2)}) collective-permute-start(f16[2056,128]{1,0:T(8,128)(2,1)S(1)} %pad_maximum_fusion), channel_id=1, source_target_pairs={{0,8},{8,0},{16,24},{24,16},{1,9},{9,1},{17,25},{25,17},{2,10},{10... | collective-permute-start | bytes 1579016 | tf_op jit(solution)/shard_map/ppermute | solution.py:291
  20.4 0.0 copy-done.2
  20.4 0.0 collective-permute-start.6
  20.4 10.4 %forward.3 = (f32[128,2048]{1,0:T(8,128)S(1)}, f32[128,2048]{1,0:T(8,128)S(1)}, f32[128,2048]{1,0:T(8,128)S(1)}, f32[8,128]{1,0:T(8,128)S(1)}) custom-call(s32[1]{0:T(128)} %bitcast.3.position_ref, bf16[128,1024]{1,0:T(8,128)(2,1)S(1)} %collective-permute-done.1.halo_ref, bf16[128,2048]{1,0:T(8,128)(2,1)S(1)} %bitcast.84, bf16[27,128,512]{2,1,0:T(8,128)(2,1)S(1)} %copy-done), custom_call_target="tpu_custom_call" | custom-call | flops 5435817984 | bytes 6684672 | tf_op jit(solution)/shard_map/forward/pallas_call | solution.py:93
  30.8 0.0 collective-permute-done.11.refs_0_
  30.8 0.0 collective-permute-done.12.refs_1_
  30.8 0.0 copy-done.1
  30.8 6.0 %backward.2.refs_5_ = f32[128,2048]{1,0:T(8,128)S(1)} custom-call(s32[1]{0:T(128)} %bitcast.3.position_ref, bf16[128,1024]{1,0:T(8,128)(2,1)S(1)} %collective-permute-done.11.refs_0_, bf16[128,1024]{1,0:T(8,128)(2,1)S(1)} %collective-permute-done.12.refs_1_, bf16[128,2048]{1,0:T(8,128)(2,1)S(1)} %bitcast.81, ...), custom_call_target="tpu_custom_call" | custom-call | flops 3623878656 | bytes 4587520 | tf_op jit(solution)/shard_map/backward/pallas_call | solution.py:168
  36.8 0.0 collective-permute-done.6
  36.9 0.1 abs_reduce_fusion
  37.0 0.1 fusion.10
  37.1 0.1 convert_element_type.161
  37.2 0.0 copy-start.3
  37.2 0.2 multiply_convert_fusion.1
  37.4 0.1 pad_maximum_fusion.3
  37.6 2.2 %collective-permute-start.7 = (f16[2056,128]{1,0:T(8,128)(2,1)S(1)}, f16[2056,128]{1,0:T(8,128)(2,1)S(1)}, u32[]{:S(2)}, u32[]{:S(2)}) collective-permute-start(f16[2056,128]{1,0:T(8,128)(2,1)S(1)} %pad_maximum_fusion.3), channel_id=1, source_target_pairs={{0,8},{8,0},{16,24},{24,16},{1,9},{9,1},{17,25},{25,17},{2,10},{10... | collective-permute-start | bytes 1579016 | tf_op jit(solution)/shard_map/ppermute | solution.py:291
  39.8 0.0 collective-permute-done.2
  39.8 0.2 fusion.1
  40.1 0.1 pad_maximum_fusion.1
  40.2 0.1 collective-permute-start.3
  40.3 0.0 copy-done.3
  40.3 0.1 broadcast_select_fusion.1.refs_2_
  40.4 0.6 collective-permute-start.9
  41.0 11.0 %collective-permute-done.7 = f16[2056,128]{1,0:T(8,128)(2,1)S(1)} collective-permute-done((f16[2056,128]{1,0:T(8,128)(2,1)S(1)}, f16[2056,128]{1,0:T(8,128)(2,1)S(1)}, u32[]{:S(2)}, u32[]{:S(2)}) %collective-permute-start.7) | collective-permute-done | bytes 526368 | tf_op jit(solution)/shard_map/ppermute | solution.py:291
  52.0 0.0 collective-permute-done.3
  52.1 0.2 fusion
  52.3 0.1 broadcast_select_fusion.refs_3_
  52.5 0.1 collective-permute-start.10
  52.5 0.1 pad_maximum_fusion.4
  52.7 0.6 collective-permute-start.8
  53.2 0.2 multiply_convert_fusion.2
  53.5 0.1 pad_maximum_fusion.2
  53.6 3.5 %collective-permute-start.4 = (f16[2056,128]{1,0:T(8,128)(2,1)S(1)}, f16[2056,128]{1,0:T(8,128)(2,1)}, u32[]{:S(2)}, u32[]{:S(2)}) collective-permute-start(f16[2056,128]{1,0:T(8,128)(2,1)S(1)} %pad_maximum_fusion.2), channel_id=1, source_target_pairs={{0,8},{8,0},{16,24},{24,16},{1,9},{9,1},{17,25},{25,17},{2,10},{10... | collective-permute-start | bytes 1579016 | tf_op jit(solution)/shard_map/ppermute | solution.py:291
  57.2 0.0 collective-permute-done.9.refs_0_
  57.2 0.0 collective-permute-done.10.refs_1_
  57.2 6.1 %backward.3 = bf16[128,2048]{1,0:T(8,128)(2,1)S(1)} custom-call(s32[1]{0:T(128)} %bitcast.3.position_ref, bf16[128,1024]{1,0:T(8,128)(2,1)S(1)} %collective-permute-done.9.refs_0_, bf16[128,1024]{1,0:T(8,128)(2,1)S(1)} %collective-permute-done.10.refs_1_, bf16[128,2048]{1,0:T(8,128)(2,1)S(1)} %broadcast_select_fusion.1.refs_2_, ...), custom_call_target="tpu_custom_call" | custom-call | flops 3623878656 | bytes 4587520 | tf_op jit(solution)/shard_map/backward/pallas_call | solution.py:168
  63.3 1.2 %reshape.101 = bf16[128,4,512]{2,1,0:T(4,128)(2,1)} reshape(bf16[128,2048]{1,0:T(8,128)(2,1)S(1)} %backward.3) | data formatting | bytes 1048576 | tf_op jit(solution)/shard_map/reshape | solution.py:356
  64.5 0.0 collective-permute-done.8
  64.5 0.7 slice_convert_fusion
  65.1 4.5 %collective-permute-done.4 = f16[2056,128]{1,0:T(8,128)(2,1)} collective-permute-done((f16[2056,128]{1,0:T(8,128)(2,1)S(1)}, f16[2056,128]{1,0:T(8,128)(2,1)}, u32[]{:S(2)}, u32[]{:S(2)}) %collective-permute-start.4) | collective-permute-done | bytes 526368 | tf_op jit(solution)/shard_map/ppermute | solution.py:291
  69.6 0.7 slice_convert_fusion.1
  70.3 1.5 %add_convert_fusion = bf16[2048,128]{1,0:T(8,128)(2,1)S(1)} fusion(f32[2048,128]{1,0:T(8,128)S(1)} %bitcast.85, f16[2056,128]{1,0:T(8,128)(2,1)} %collective-permute-done.8, f16[2056,128]{1,0:T(8,128)(2,1)} %collective-permute-done.4, f32[128]{0:T(128)S(1)} %multiply_bitcast_fusion, f32[128]{0:T(128)S(1)} %multiply_bitcast_fusion.2, pred[]{:T(512)S(6)} %or.3), kind=kLoop, calls=%fused_computation | loop fusion | flops 2097152 | bytes 2622465 | tf_op jit(solution)/shard_map/convert_element_type | solution.py:355
  71.8 0.1 copy.6
  71.9 1.0 %reshape_reshape.3 = bf16[128,4,512]{2,1,0:T(4,128)(2,1)} reshape(bf16[16,8,16,128]{3,2,1,0:T(8,128)(2,1)S(1)} %copy.6) | data formatting | bytes 1048576 | tf_op jit(solution)/shard_map/reshape;reshape | solution.py:356
  (27 shorter events, 0.4 us)
Async XLA Ops:
  1.8 15.0 %collective-permute-start.5 = (bf16[128,2048]{1,0:T(8,128)(2,1)S(1)}, bf16[128,2048]{1,0:T(8,128)(2,1)S(1)}, u32[]{:S(2)}, u32[]{:S(2)}) collective-permute-start(bf16[128,2048]{1,0:T(8,128)(2,1)S(1)} %bitcast.78), channel_id=1, source_target_pairs={{0,8},{8,0},{16,24},{24,16},{1,9},{9,1},{17,25},{25,17},{2,10},{10... | collective-permute-start | bytes 1572872 | tf_op jit(solution)/shard_map/ppermute | solution.py:291
  4.9 12.1 %collective-permute-start = (bf16[128,2048]{1,0:T(8,128)(2,1)S(1)}, bf16[128,2048]{1,0:T(8,128)(2,1)S(1)}, u32[]{:S(2)}, u32[]{:S(2)}) collective-permute-start(bf16[128,2048]{1,0:T(8,128)(2,1)S(1)} %bitcast.79), channel_id=1, source_target_pairs={{8,16},{16,8},{0,4},{24,28},{12,20},{20,12},{4,0},{28,24},{9,17},{... | collective-permute-start | bytes 1572872 | tf_op jit(solution)/shard_map/ppermute | solution.py:299
  6.1 1.7 %collective-permute-start.1 = (bf16[128,1024]{1,0:T(8,128)(2,1)S(1)}, bf16[128,1024]{1,0:T(8,128)(2,1)S(1)}, u32[]{:S(2)}, u32[]{:S(2)}) collective-permute-start(bf16[128,1024]{1,0:T(8,128)(2,1)S(1)} %pad_maximum_fusion.5), channel_id=1, source_target_pairs={{0,4},{4,0},{1,5},{5,1},{2,6},{6,2},{3,7},{7,3},{8,12},{12,8},{9,1... | collective-permute-start | bytes 786440 | tf_op jit(solution)/shard_map/ppermute | solution.py:246
  6.7 24.0 %collective-permute-start.11 = (bf16[128,1024]{1,0:T(8,128)(2,1)S(1)}, bf16[128,1024]{1,0:T(8,128)(2,1)S(1)}, u32[]{:S(2)}, u32[]{:S(2)}) collective-permute-start(bf16[128,1024]{1,0:T(8,128)(2,1)S(1)} %pad_maximum_fusion.8), channel_id=1, source_target_pairs={{0,4},{4,0},{1,5},{5,1},{2,6},{6,2},{3,7},{7,3},{8,12},{12,8},{9,1... | collective-permute-start | bytes 786440 | tf_op jit(solution)/shard_map/ppermute | solution.py:246
  7.8 2.0 %copy-start = (bf16[27,128,512]{2,1,0:T(8,128)(2,1)S(1)}, bf16[27,128,512]{2,1,0:T(8,128)(2,1)}, u32[]{:S(2)}) copy-start(bf16[27,128,512]{2,1,0:T(8,128)(2,1)} %refs_4_.3) | copy-start | bytes 10616836
  16.9 13.9 %collective-permute-start.12 = (bf16[128,1024]{1,0:T(8,128)(2,1)S(1)}, bf16[128,1024]{1,0:T(8,128)(2,1)S(1)}, u32[]{:S(2)}, u32[]{:S(2)}) collective-permute-start(bf16[128,1024]{1,0:T(8,128)(2,1)S(1)} %pad_maximum_fusion.9), channel_id=1, source_target_pairs={{0,4},{4,0},{1,5},{5,1},{2,6},{6,2},{3,7},{7,3},{8,12},{12,8},{9,1... | collective-permute-start | bytes 786440 | tf_op jit(solution)/shard_map/ppermute | solution.py:246
  17.0 3.4 %copy-start.2 = (bf16[128,2048]{1,0:T(8,128)(2,1)}, bf16[128,2048]{1,0:T(8,128)(2,1)S(1)}, u32[]{:S(2)}) copy-start(bf16[128,2048]{1,0:T(8,128)(2,1)S(1)} %collective-permute-done) | copy-start | bytes 1572868
  17.6 13.2 %copy-start.1 = (bf16[27,128,512]{2,1,0:T(8,128)(2,1)S(1)}, bf16[27,128,512]{2,1,0:T(8,128)(2,1)}, u32[]{:S(2)}) copy-start(bf16[27,128,512]{2,1,0:T(8,128)(2,1)} %refs_4_.3) | copy-start | bytes 10616836
  17.6 22.2 %collective-permute-start.2 = (f16[2056,128]{1,0:T(8,128)(2,1)S(1)}, f16[2056,128]{1,0:T(8,128)(2,1)S(1)}, u32[]{:S(2)}, u32[]{:S(2)}) collective-permute-start(f16[2056,128]{1,0:T(8,128)(2,1)S(1)} %pad_maximum_fusion), channel_id=1, source_target_pairs={{0,8},{8,0},{16,24},{24,16},{1,9},{9,1},{17,25},{25,17},{2,10},{10... | collective-permute-start | bytes 1579016 | tf_op jit(solution)/shard_map/ppermute | solution.py:291
  20.4 16.5 %collective-permute-start.6 = (bf16[128,2048]{1,0:T(8,128)(2,1)S(1)}, bf16[128,2048]{1,0:T(8,128)(2,1)S(1)}, u32[]{:S(2)}, u32[]{:S(2)}) collective-permute-start(bf16[128,2048]{1,0:T(8,128)(2,1)S(1)} %collective-permute-done.5.refs_3_), channel_id=1, source_target_pairs={{8,16},{16,8},{0,4},{24,28},{12,20},{20,12},{4,0},{28,24},{9,17},{... | collective-permute-start | bytes 1572872 | tf_op jit(solution)/shard_map/ppermute | solution.py:299
  37.2 3.1 %copy-start.3 = (bf16[128,2048]{1,0:T(8,128)(2,1)S(1)}, bf16[128,2048]{1,0:T(8,128)(2,1)}, u32[]{:S(2)}) copy-start(bf16[128,2048]{1,0:T(8,128)(2,1)} %copy-done.2) | copy-start | bytes 1572868
  37.6 14.4 %collective-permute-start.7 = (f16[2056,128]{1,0:T(8,128)(2,1)S(1)}, f16[2056,128]{1,0:T(8,128)(2,1)S(1)}, u32[]{:S(2)}, u32[]{:S(2)}) collective-permute-start(f16[2056,128]{1,0:T(8,128)(2,1)S(1)} %pad_maximum_fusion.3), channel_id=1, source_target_pairs={{0,8},{8,0},{16,24},{24,16},{1,9},{9,1},{17,25},{25,17},{2,10},{10... | collective-permute-start | bytes 1579016 | tf_op jit(solution)/shard_map/ppermute | solution.py:291
  40.2 11.8 %collective-permute-start.3 = (f16[2056,128]{1,0:T(8,128)(2,1)S(1)}, f16[2056,128]{1,0:T(8,128)(2,1)S(1)}, u32[]{:S(2)}, u32[]{:S(2)}) collective-permute-start(f16[2056,128]{1,0:T(8,128)(2,1)S(1)} %pad_maximum_fusion.1), channel_id=1, source_target_pairs={{8,16},{16,8},{0,4},{24,28},{12,20},{20,12},{4,0},{28,24},{9,17},{... | collective-permute-start | bytes 1579016 | tf_op jit(solution)/shard_map/ppermute | solution.py:299
  40.4 16.7 %collective-permute-start.9 = (bf16[128,1024]{1,0:T(8,128)(2,1)S(1)}, bf16[128,1024]{1,0:T(8,128)(2,1)S(1)}, u32[]{:S(2)}, u32[]{:S(2)}) collective-permute-start(bf16[128,1024]{1,0:T(8,128)(2,1)S(1)} %pad_maximum_fusion.6), channel_id=1, source_target_pairs={{0,4},{4,0},{1,5},{5,1},{2,6},{6,2},{3,7},{7,3},{8,12},{12,8},{9,1... | collective-permute-start | bytes 786440 | tf_op jit(solution)/shard_map/ppermute | solution.py:246
  52.5 4.7 %collective-permute-start.10 = (bf16[128,1024]{1,0:T(8,128)(2,1)S(1)}, bf16[128,1024]{1,0:T(8,128)(2,1)S(1)}, u32[]{:S(2)}, u32[]{:S(2)}) collective-permute-start(bf16[128,1024]{1,0:T(8,128)(2,1)S(1)} %pad_maximum_fusion.7), channel_id=1, source_target_pairs={{0,4},{4,0},{1,5},{5,1},{2,6},{6,2},{3,7},{7,3},{8,12},{12,8},{9,1... | collective-permute-start | bytes 786440 | tf_op jit(solution)/shard_map/ppermute | solution.py:246
  52.7 11.8 %collective-permute-start.8 = (f16[2056,128]{1,0:T(8,128)(2,1)S(1)}, f16[2056,128]{1,0:T(8,128)(2,1)}, u32[]{:S(2)}, u32[]{:S(2)}) collective-permute-start(f16[2056,128]{1,0:T(8,128)(2,1)S(1)} %pad_maximum_fusion.4), channel_id=1, source_target_pairs={{8,16},{16,8},{0,4},{24,28},{12,20},{20,12},{4,0},{28,24},{9,17},{... | collective-permute-start | bytes 1579016 | tf_op jit(solution)/shard_map/ppermute | solution.py:299
  53.6 16.0 %collective-permute-start.4 = (f16[2056,128]{1,0:T(8,128)(2,1)S(1)}, f16[2056,128]{1,0:T(8,128)(2,1)}, u32[]{:S(2)}, u32[]{:S(2)}) collective-permute-start(f16[2056,128]{1,0:T(8,128)(2,1)S(1)} %pad_maximum_fusion.2), channel_id=1, source_target_pairs={{0,8},{8,0},{16,24},{24,16},{1,9},{9,1},{17,25},{25,17},{2,10},{10... | collective-permute-start | bytes 1579016 | tf_op jit(solution)/shard_map/ppermute | solution.py:291

commit v4 on v3

--- a/solution.py
+++ b/solution.py
@@ -122,7 +122,7 @@
     before = None if first else refs[2 * number + 1]
     out_ref, lhs, rhs = refs[-3:]
     plane = pl.program_id(0)
-    chans_in, size = w_ref.shape[1], out_ref.shape[1]
+    chans_in, size = w_ref.shape[1], blocks[0].shape[1] // slab
     chans = blocks[0].shape[0]
 
     @pl.when(plane == 0)
@@ -153,7 +153,15 @@
             over_y = part if over_y is None else over_y + part
         over_y = shift_z(over_y, offset_z)
         total = over_y if total is None else total + over_y
-    out_ref[...] = total.astype(out_ref.dtype)
+    value = total.astype(out_ref.dtype)
+    if first:
+        out_ref[...] = value
+    else:
+        for p in range(slab):
+
+            @pl.when(plane == p)
+            def _():
+                out_ref[:, p, :] = value
 
 
 def backward(position, sources, blocks, halos, w, before, slab, out_dtype):
@@ -164,16 +172,17 @@
     first = before is None
     whole = lambda a: pl.BlockSpec(a.shape, lambda n, s: (0,) * a.ndim, pipeline_mode=pl.Buffered(1))
     each = pl.BlockSpec((chans_in, size), lambda n, s: (0, n))
+    out = jax.ShapeDtypeStruct((chans_in, cells) if first else (chans_in, slab, size), out_dtype)
     args = (*halos, *blocks, w) + (() if first else (before,))
     return pl.pallas_call(
         functools.partial(backward_kernel, slab, sources, first),
         grid_spec=pltpu.PrefetchScalarGridSpec(
             num_scalar_prefetch=1, grid=(slab,),
             in_specs=[whole(a) for a in args[:2 * number + 1]] + ([] if first else [each]),
-            out_specs=each,
+            out_specs=each if first else whole(out),
             scratch_shapes=[pltpu.VMEM((9 * chans_in, 3 * number * chans), jnp.bfloat16),
                             pltpu.VMEM((3 * number * chans, cells), jnp.bfloat16)]),
-        out_shape=jax.ShapeDtypeStruct((chans_in, cells), out_dtype),
+        out_shape=out,
         compiler_params=pltpu.CompilerParams(vmem_limit_bytes=BACKWARD_VMEM),
         cost_estimate=pl.CostEstimate(flops=2*27*chans*chans_in*cells*number, bytes_accessed=w.size*2+chans_in*cells*4, transcendentals=0),
         name="backward",
@@ -343,8 +352,10 @@
     grad_2 = jnp.where(inner, middle_1, cotangent_of(ends_2))
     edges_2 = edge_planes(grad_2, size)
 
-    ends_4 = swap_ends(sum_with(third, marks, middle_3, inner))
+    parcel = sum_with(third, marks, middle_3, inner)
+    ends_4 = swap_ends(parcel)
     middle_4 = swap_middle(sum_with(second, marks, ends_3))
+    _, ends_3, middle_2 = lax.optimization_barrier((parcel, ends_3, middle_2))
     grad_3 = jnp.where(inner, middle_2, cotangent_of(ends_3))
     edges_3 = edge_planes(grad_3, size)
     input_grad = backward(
@@ -353,7 +364,7 @@
     )
     conv_out = own + unpack(ends_4) + jnp.where(inner, unpack(middle_4), 0.0)
     conv_out = untiled(conv_out.astype(jnp.bfloat16), chans)
-    return conv_out.reshape(shape), input_grad.reshape(shape)
+    return conv_out.reshape(shape), input_grad
 
 
 def first_sum(place):

time: 73.2 us -> 68.7 us (0.939); the launches traced: 72.9 us -> 67.5 us
  other arithmetic: 5.55 us -> 3.11 us
  waiting for transfers between devices: 17.7 us -> 16.1 us
  starting transfers between devices: 13.7 us -> 12.4 us
  local copies, waits for them, and re-layouts: 6.68 us -> 5.5 us
  Pallas kernels: 28.3 us -> 29.4 us
    ppermute x4, waiting for transfers between devices: 16.7 us -> 14.5 us  [swap_ends(): return lax.ppermute(block, 'chan', [(0, 1), (1, 0), (2, 3), (3, 2)])]
    convert_element_type x6 -> x7, other arithmetic: 1.51 us -> 0.18 us  [scale_of(): marks = marks.astype(jnp.float32)]
    ppermute x4, starting transfers between devices: 11.7 us -> 10.4 us  [swap_ends(): return lax.ppermute(block, 'chan', [(0, 1), (1, 0), (2, 3), (3, 2)])]
    convert_element_type x1, other arithmetic: 1.48 us -> 0.3 us  [line_of_four(): conv_out = untiled(conv_out.astype(jnp.bfloat16), chans)]
    reshape x1 -> x0, local copies, waits for them, and re-layouts: 1.17 us -> none  [line_of_four(): return (conv_out.reshape(shape), input_grad.reshape(shape))]
    pallas_call x2, Pallas kernels: 12.1 us -> 13.3 us  [backward(): pl.pallas_call(functools.partial(backward_kernel, slab, sources, first),...]
    unnamed x10 -> x6, local copies, waits for them, and re-layouts: 4.3 us -> 4.29 us
  transfers between devices with their start and end apart: 13 -> 13, of which waited for: 4 -> 5; matrix products, arithmetic and copies ran while one was open for 8% -> 6% of each run, Pallas kernels for 39% -> 44%
where the time goes in v4:
time: 68.7 us; the launch traced here: 67.5 us
  Pallas kernels  29.4 us (43%)
  waiting for transfers between devices  16.1 us (23%)
  starting transfers between devices  12.4 us (18%)
  local copies, waits for them, and re-layouts  5.5 us (8%)
  other arithmetic  3.11 us (5%)
  between operations  1.01 us (1%)
    pallas_call x2, Pallas kernels, forward(): pl.pallas_call(functools.partial(forward_kernel, slab, sums), grid_spec=p...  16.1 us
    ppermute x4, waiting for transfers between devices, swap_ends(): return lax.ppermute(block, 'chan', [(0, 1), (1, 0), (2, 3), (3, 2)])  14.5 us
    pallas_call x2, Pallas kernels, backward(): pl.pallas_call(functools.partial(backward_kernel, slab, sources, first),...  13.3 us
    ppermute x4, starting transfers between devices, swap_ends(): return lax.ppermute(block, 'chan', [(0, 1), (1, 0), (2, 3), (3, 2)])  10.4 us
    unnamed x6, local copies, waits for them, and re-layouts  4.29 us
    ppermute x5, waiting for transfers between devices, edge_planes(): return lax.ppermute(jnp.concatenate([last, first], axis=1), 'slab', upward)  1.59 us
  transfers between devices with their start and end apart: 13, of which 5 were waited for; matrix products, arithmetic and copies ran while one was open for 6% of the time, Pallas kernels for 44%

profile of v4, /device:TPU:0, one launch (start us, length us, event | category | flops | bytes accessed | tf_op | source)
XLA Modules:
  0.0 67.5 jit_solution(16059650524061184294)
XLA Ops:
  0.6 1.1 %copy.7 = bf16[16,8,4,512]{3,1,2,0:T(8,128)(2,1)S(1)} copy(bf16[16,8,4,512]{3,2,1,0:T(4,128)(2,1)} %bitcast.94) | data formatting | bytes 1048576
  1.8 3.1 %collective-permute-start.5 = (bf16[128,2048]{1,0:T(8,128)(2,1)S(1)}, bf16[128,2048]{1,0:T(8,128)(2,1)S(1)}, u32[]{:S(2)}, u32[]{:S(2)}) collective-permute-start(bf16[128,2048]{1,0:T(8,128)(2,1)S(1)} %bitcast.80), channel_id=1, source_target_pairs={{0,8},{8,0},{16,24},{24,16},{1,9},{9,1},{17,25},{25,17},{2,10},{10... | collective-permute-start | bytes 1572872 | tf_op jit(solution)/shard_map/ppermute | solution.py:300
  4.9 0.0 collective-permute-start
  4.9 1.1 %copy.8 = bf16[16,8,4,512]{3,1,2,0:T(8,128)(2,1)S(1)} copy(bf16[16,8,4,512]{3,2,1,0:T(4,128)(2,1)} %bitcast.95) | data formatting | bytes 1048576
  6.1 0.6 collective-permute-start.1
  6.7 0.1 collective-permute-start.11
  6.8 1.0 %collective-permute-done.1.halo_ref = bf16[128,1024]{1,0:T(8,128)(2,1)S(1)} collective-permute-done((bf16[128,1024]{1,0:T(8,128)(2,1)S(1)}, bf16[128,1024]{1,0:T(8,128)(2,1)S(1)}, u32[]{:S(2)}, u32[]{:S(2)}) %collective-permute-start.1) | collective-permute-done | bytes 262176 | tf_op jit(solution)/shard_map/ppermute | solution.py:255
  7.8 0.0 copy-start
  7.8 2.0 %copy-done = bf16[27,128,512]{2,1,0:T(8,128)(2,1)S(1)} copy-done((bf16[27,128,512]{2,1,0:T(8,128)(2,1)S(1)}, bf16[27,128,512]{2,1,0:T(8,128)(2,1)}, u32[]{:S(2)}) %copy-start) | copy-done | bytes 3538968
  9.8 5.7 %forward.2 = (f32[128,2048]{1,0:T(8,128)S(1)}, f32[8,128]{1,0:T(8,128)S(1)}) custom-call(s32[1]{0:T(128)} %bitcast.3.position_ref, bf16[128,1024]{1,0:T(8,128)(2,1)S(1)} %collective-permute-done.1.halo_ref, bf16[128,2048]{1,0:T(8,128)(2,1)S(1)} %bitcast.85, bf16[27,128,512]{2,1,0:T(8,128)(2,1)S(1)} %copy-done), custom_call_target="tpu_custom_call" | custom-call | flops 1811939328 | bytes 4587520 | tf_op jit(solution)/shard_map/forward/pallas_call | solution.py:93
  15.6 1.2 %collective-permute-done.5.refs_3_ = bf16[128,2048]{1,0:T(8,128)(2,1)S(1)} collective-permute-done((bf16[128,2048]{1,0:T(8,128)(2,1)S(1)}, bf16[128,2048]{1,0:T(8,128)(2,1)S(1)}, u32[]{:S(2)}, u32[]{:S(2)}) %collective-permute-start.5) | collective-permute-done | bytes 524320 | tf_op jit(solution)/shard_map/ppermute | solution.py:300
  16.9 0.1 collective-permute-start.12
  16.9 0.0 collective-permute-done
  17.0 0.1 abs_reduce_fusion.1
  17.1 0.1 fusion.11
  17.2 0.1 convert_element_type.166
  17.3 0.2 multiply_convert_fusion.5
  17.4 0.1 pad_maximum_fusion
  17.6 0.0 copy-start.1
  17.6 2.8 %collective-permute-start.2 = (f16[2056,128]{1,0:T(8,128)(2,1)S(1)}, f16[2056,128]{1,0:T(8,128)(2,1)S(1)}, u32[]{:S(2)}, u32[]{:S(2)}) collective-permute-start(f16[2056,128]{1,0:T(8,128)(2,1)S(1)} %pad_maximum_fusion), channel_id=1, source_target_pairs={{0,8},{8,0},{16,24},{24,16},{1,9},{9,1},{17,25},{25,17},{2,10},{10... | collective-permute-start | bytes 1579016 | tf_op jit(solution)/shard_map/ppermute | solution.py:300
  20.4 0.0 collective-permute-start.6
  20.4 10.4 %forward.3 = (f32[128,2048]{1,0:T(8,128)S(1)}, f32[128,2048]{1,0:T(8,128)S(1)}, f32[128,2048]{1,0:T(8,128)S(1)}, f32[8,128]{1,0:T(8,128)S(1)}) custom-call(s32[1]{0:T(128)} %bitcast.3.position_ref, bf16[128,1024]{1,0:T(8,128)(2,1)S(1)} %collective-permute-done.1.halo_ref, bf16[128,2048]{1,0:T(8,128)(2,1)S(1)} %bitcast.86, bf16[27,128,512]{2,1,0:T(8,128)(2,1)S(1)} %copy-done), custom_call_target="tpu_custom_call" | custom-call | flops 5435817984 | bytes 6684672 | tf_op jit(solution)/shard_map/forward/pallas_call | solution.py:93
  30.8 0.0 collective-permute-done.11.refs_0_
  30.8 0.0 collective-permute-done.12.refs_1_
  30.8 0.0 copy-done.1
  30.8 6.0 %backward.2.refs_5_ = f32[128,2048]{1,0:T(8,128)S(1)} custom-call(s32[1]{0:T(128)} %bitcast.3.position_ref, bf16[128,1024]{1,0:T(8,128)(2,1)S(1)} %collective-permute-done.11.refs_0_, bf16[128,1024]{1,0:T(8,128)(2,1)S(1)} %collective-permute-done.12.refs_1_, bf16[128,2048]{1,0:T(8,128)(2,1)S(1)} %bitcast.83, ...), custom_call_target="tpu_custom_call" | custom-call | flops 3623878656 | bytes 4587520 | tf_op jit(solution)/shard_map/backward/pallas_call | solution.py:177
  36.8 0.0 collective-permute-done.6
  36.8 0.1 abs_reduce_fusion
  37.0 0.1 fusion.9
  37.0 0.1 convert_element_type.167
  37.2 0.2 multiply_convert_fusion.2
  37.4 0.1 pad_maximum_fusion.3
  37.5 2.2 %collective-permute-start.7 = (f16[2056,128]{1,0:T(8,128)(2,1)S(1)}, f16[2056,128]{1,0:T(8,128)(2,1)S(1)}, u32[]{:S(2)}, u32[]{:S(2)}) collective-permute-start(f16[2056,128]{1,0:T(8,128)(2,1)S(1)} %pad_maximum_fusion.3), channel_id=1, source_target_pairs={{0,8},{8,0},{16,24},{24,16},{1,9},{9,1},{17,25},{25,17},{2,10},{10... | collective-permute-start | bytes 1579016 | tf_op jit(solution)/shard_map/ppermute | solution.py:300
  39.8 0.0 collective-permute-done.2
  39.8 0.2 fusion
  40.0 0.1 pad_maximum_fusion.1
  40.2 0.1 collective-permute-start.3
  40.3 0.1 broadcast_select_fusion.1.refs_2_
  40.4 0.6 collective-permute-start.9
  41.0 11.0 %collective-permute-done.7 = f16[2056,128]{1,0:T(8,128)(2,1)S(1)} collective-permute-done((f16[2056,128]{1,0:T(8,128)(2,1)S(1)}, f16[2056,128]{1,0:T(8,128)(2,1)S(1)}, u32[]{:S(2)}, u32[]{:S(2)}) %collective-permute-start.7) | collective-permute-done | bytes 526368 | tf_op jit(solution)/shard_map/ppermute | solution.py:300
  52.0 0.0 collective-permute-done.3
  52.1 0.2 multiply_convert_fusion.3
  52.3 0.1 pad_maximum_fusion.2
  52.4 2.3 %collective-permute-start.4 = (f16[2056,128]{1,0:T(8,128)(2,1)S(1)}, f16[2056,128]{1,0:T(8,128)(2,1)S(1)}, u32[]{:S(2)}, u32[]{:S(2)}) collective-permute-start(f16[2056,128]{1,0:T(8,128)(2,1)S(1)} %pad_maximum_fusion.2), channel_id=1, source_target_pairs={{0,8},{8,0},{16,24},{24,16},{1,9},{9,1},{17,25},{25,17},{2,10},{10... | collective-permute-start | bytes 1579016 | tf_op jit(solution)/shard_map/ppermute | solution.py:300
  54.7 0.1 multiply_convert_fusion
  54.8 0.1 broadcast_select_fusion.refs_3_
  55.0 0.1 collective-permute-start.10
  55.0 0.2 multiply_convert_fusion.1
  55.3 0.1 pad_maximum_fusion.4
  55.4 0.6 collective-permute-start.8
  56.0 0.0 collective-permute-done.9.refs_0_
  56.0 0.6 collective-permute-done.10.refs_1_
  56.6 7.2 %backward.3 = bf16[128,4,512]{2,1,0:T(4,128)(2,1)} custom-call(s32[1]{0:T(128)} %bitcast.3.position_ref, bf16[128,1024]{1,0:T(8,128)(2,1)S(1)} %collective-permute-done.9.refs_0_, bf16[128,1024]{1,0:T(8,128)(2,1)S(1)} %collective-permute-done.10.refs_1_, bf16[128,2048]{1,0:T(8,128)(2,1)S(1)} %broadcast_select_fusion.1.refs_2_, ...), custom_call_target="tpu_custom_call" | custom-call | flops 3623878656 | bytes 4587520 | tf_op jit(solution)/shard_map/backward/pallas_call | solution.py:177
  63.8 2.2 %collective-permute-done.4 = f16[2056,128]{1,0:T(8,128)(2,1)S(1)} collective-permute-done((f16[2056,128]{1,0:T(8,128)(2,1)S(1)}, f16[2056,128]{1,0:T(8,128)(2,1)S(1)}, u32[]{:S(2)}, u32[]{:S(2)}) %collective-permute-start.4) | collective-permute-done | bytes 526368 | tf_op jit(solution)/shard_map/ppermute | solution.py:300
  66.1 0.0 collective-permute-done.8
  66.1 0.3 add_convert_fusion
  66.4 0.1 copy.6
  66.5 1.0 %reshape_reshape.3 = bf16[128,4,512]{2,1,0:T(4,128)(2,1)} reshape(bf16[16,8,16,128]{3,2,1,0:T(8,128)(2,1)S(1)} %copy.6) | data formatting | bytes 1048576 | tf_op jit(solution)/shard_map/reshape;reshape | solution.py:367
  (31 shorter events, 0.4 us)
Async XLA Ops:
  1.8 15.0 %collective-permute-start.5 = (bf16[128,2048]{1,0:T(8,128)(2,1)S(1)}, bf16[128,2048]{1,0:T(8,128)(2,1)S(1)}, u32[]{:S(2)}, u32[]{:S(2)}) collective-permute-start(bf16[128,2048]{1,0:T(8,128)(2,1)S(1)} %bitcast.80), channel_id=1, source_target_pairs={{0,8},{8,0},{16,24},{24,16},{1,9},{9,1},{17,25},{25,17},{2,10},{10... | collective-permute-start | bytes 1572872 | tf_op jit(solution)/shard_map/ppermute | solution.py:300
  4.9 12.1 %collective-permute-start = (bf16[128,2048]{1,0:T(8,128)(2,1)S(1)}, bf16[128,2048]{1,0:T(8,128)(2,1)S(1)}, u32[]{:S(2)}, u32[]{:S(2)}) collective-permute-start(bf16[128,2048]{1,0:T(8,128)(2,1)S(1)} %bitcast.81), channel_id=1, source_target_pairs={{8,16},{16,8},{0,4},{24,28},{12,20},{20,12},{4,0},{28,24},{9,17},{... | collective-permute-start | bytes 1572872 | tf_op jit(solution)/shard_map/ppermute | solution.py:308
  6.1 1.7 %collective-permute-start.1 = (bf16[128,1024]{1,0:T(8,128)(2,1)S(1)}, bf16[128,1024]{1,0:T(8,128)(2,1)S(1)}, u32[]{:S(2)}, u32[]{:S(2)}) collective-permute-start(bf16[128,1024]{1,0:T(8,128)(2,1)S(1)} %pad_maximum_fusion.5), channel_id=1, source_target_pairs={{0,4},{4,0},{1,5},{5,1},{2,6},{6,2},{3,7},{7,3},{8,12},{12,8},{9,1... | collective-permute-start | bytes 786440 | tf_op jit(solution)/shard_map/ppermute | solution.py:255
  6.7 24.0 %collective-permute-start.11 = (bf16[128,1024]{1,0:T(8,128)(2,1)S(1)}, bf16[128,1024]{1,0:T(8,128)(2,1)S(1)}, u32[]{:S(2)}, u32[]{:S(2)}) collective-permute-start(bf16[128,1024]{1,0:T(8,128)(2,1)S(1)} %pad_maximum_fusion.8), channel_id=1, source_target_pairs={{0,4},{4,0},{1,5},{5,1},{2,6},{6,2},{3,7},{7,3},{8,12},{12,8},{9,1... | collective-permute-start | bytes 786440 | tf_op jit(solution)/shard_map/ppermute | solution.py:255
  7.8 2.0 %copy-start = (bf16[27,128,512]{2,1,0:T(8,128)(2,1)S(1)}, bf16[27,128,512]{2,1,0:T(8,128)(2,1)}, u32[]{:S(2)}) copy-start(bf16[27,128,512]{2,1,0:T(8,128)(2,1)} %refs_4_.3) | copy-start | bytes 10616836
  16.9 13.9 %collective-permute-start.12 = (bf16[128,1024]{1,0:T(8,128)(2,1)S(1)}, bf16[128,1024]{1,0:T(8,128)(2,1)S(1)}, u32[]{:S(2)}, u32[]{:S(2)}) collective-permute-start(bf16[128,1024]{1,0:T(8,128)(2,1)S(1)} %pad_maximum_fusion.9), channel_id=1, source_target_pairs={{0,4},{4,0},{1,5},{5,1},{2,6},{6,2},{3,7},{7,3},{8,12},{12,8},{9,1... | collective-permute-start | bytes 786440 | tf_op jit(solution)/shard_map/ppermute | solution.py:255
  17.6 13.2 %copy-start.1 = (bf16[27,128,512]{2,1,0:T(8,128)(2,1)S(1)}, bf16[27,128,512]{2,1,0:T(8,128)(2,1)}, u32[]{:S(2)}) copy-start(bf16[27,128,512]{2,1,0:T(8,128)(2,1)} %refs_4_.3) | copy-start | bytes 10616836
  17.6 22.2 %collective-permute-start.2 = (f16[2056,128]{1,0:T(8,128)(2,1)S(1)}, f16[2056,128]{1,0:T(8,128)(2,1)S(1)}, u32[]{:S(2)}, u32[]{:S(2)}) collective-permute-start(f16[2056,128]{1,0:T(8,128)(2,1)S(1)} %pad_maximum_fusion), channel_id=1, source_target_pairs={{0,8},{8,0},{16,24},{24,16},{1,9},{9,1},{17,25},{25,17},{2,10},{10... | collective-permute-start | bytes 1579016 | tf_op jit(solution)/shard_map/ppermute | solution.py:300
  20.4 16.4 %collective-permute-start.6 = (bf16[128,2048]{1,0:T(8,128)(2,1)S(1)}, bf16[128,2048]{1,0:T(8,128)(2,1)S(1)}, u32[]{:S(2)}, u32[]{:S(2)}) collective-permute-start(bf16[128,2048]{1,0:T(8,128)(2,1)S(1)} %collective-permute-done.5.refs_3_), channel_id=1, source_target_pairs={{8,16},{16,8},{0,4},{24,28},{12,20},{20,12},{4,0},{28,24},{9,17},{... | collective-permute-start | bytes 1572872 | tf_op jit(solution)/shard_map/ppermute | solution.py:308
  37.5 14.4 %collective-permute-start.7 = (f16[2056,128]{1,0:T(8,128)(2,1)S(1)}, f16[2056,128]{1,0:T(8,128)(2,1)S(1)}, u32[]{:S(2)}, u32[]{:S(2)}) collective-permute-start(f16[2056,128]{1,0:T(8,128)(2,1)S(1)} %pad_maximum_fusion.3), channel_id=1, source_target_pairs={{0,8},{8,0},{16,24},{24,16},{1,9},{9,1},{17,25},{25,17},{2,10},{10... | collective-permute-start | bytes 1579016 | tf_op jit(solution)/shard_map/ppermute | solution.py:300
  40.2 11.8 %collective-permute-start.3 = (f16[2056,128]{1,0:T(8,128)(2,1)S(1)}, f16[2056,128]{1,0:T(8,128)(2,1)S(1)}, u32[]{:S(2)}, u32[]{:S(2)}) collective-permute-start(f16[2056,128]{1,0:T(8,128)(2,1)S(1)} %pad_maximum_fusion.1), channel_id=1, source_target_pairs={{8,16},{16,8},{0,4},{24,28},{12,20},{20,12},{4,0},{28,24},{9,17},{... | collective-permute-start | bytes 1579016 | tf_op jit(solution)/shard_map/ppermute | solution.py:308
  40.4 15.6 %collective-permute-start.9 = (bf16[128,1024]{1,0:T(8,128)(2,1)S(1)}, bf16[128,1024]{1,0:T(8,128)(2,1)S(1)}, u32[]{:S(2)}, u32[]{:S(2)}) collective-permute-start(bf16[128,1024]{1,0:T(8,128)(2,1)S(1)} %pad_maximum_fusion.6), channel_id=1, source_target_pairs={{0,4},{4,0},{1,5},{5,1},{2,6},{6,2},{3,7},{7,3},{8,12},{12,8},{9,1... | collective-permute-start | bytes 786440 | tf_op jit(solution)/shard_map/ppermute | solution.py:255
  52.4 13.6 %collective-permute-start.4 = (f16[2056,128]{1,0:T(8,128)(2,1)S(1)}, f16[2056,128]{1,0:T(8,128)(2,1)S(1)}, u32[]{:S(2)}, u32[]{:S(2)}) collective-permute-start(f16[2056,128]{1,0:T(8,128)(2,1)S(1)} %pad_maximum_fusion.2), channel_id=1, source_target_pairs={{0,8},{8,0},{16,24},{24,16},{1,9},{9,1},{17,25},{25,17},{2,10},{10... | collective-permute-start | bytes 1579016 | tf_op jit(solution)/shard_map/ppermute | solution.py:300
  55.0 1.6 %collective-permute-start.10 = (bf16[128,1024]{1,0:T(8,128)(2,1)S(1)}, bf16[128,1024]{1,0:T(8,128)(2,1)S(1)}, u32[]{:S(2)}, u32[]{:S(2)}) collective-permute-start(bf16[128,1024]{1,0:T(8,128)(2,1)S(1)} %pad_maximum_fusion.7), channel_id=1, source_target_pairs={{0,4},{4,0},{1,5},{5,1},{2,6},{6,2},{3,7},{7,3},{8,12},{12,8},{9,1... | collective-permute-start | bytes 786440 | tf_op jit(solution)/shard_map/ppermute | solution.py:255
  55.4 10.7 %collective-permute-start.8 = (f16[2056,128]{1,0:T(8,128)(2,1)S(1)}, f16[2056,128]{1,0:T(8,128)(2,1)S(1)}, u32[]{:S(2)}, u32[]{:S(2)}) collective-permute-start(f16[2056,128]{1,0:T(8,128)(2,1)S(1)} %pad_maximum_fusion.4), channel_id=1, source_target_pairs={{8,16},{16,8},{0,4},{24,28},{12,20},{20,12},{4,0},{28,24},{9,17},{... | collective-permute-start | bytes 1579016 | tf_op jit(solution)/shard_map/ppermute | solution.py:308
